TPU v7x, 32 devices: a whole 2x2x4 slice. The times are simulated.
32 devices in a mesh: groups: 2 (over x), dp: 8 (over z, y), mp: 2 (over core).
Axes of the slice: x: 2, y: 2, z: 4, core: 2. Of those that a mesh axis runs over, the one named last changes fastest.
Arguments:
- residual: bfloat16 [48, 128, 8192], P(('groups', 'dp'), None, 'mp'), parts along dimension 0
- lengths: int32 [48], P(('groups', 'dp')), parts along dimension 0, may hold values from 32 to 128
- labels: int32 [48], P(('groups', 'dp')), parts along dimension 0, may hold values from 0 to 1, as said below
- earlier_means: float32 [16, 79, 2, 8192], P(('groups', 'dp'), None, None, 'mp'), parts along dimension 0
- chosen: int32 [2], P('groups'), parts along dimension 0, may hold values from 0 to 79
- norm_gain: float32 [8192], P('mp'), may hold values from 0.1 to 1.9
- key_weight: bfloat16 [2, 4096, 1024], P('mp', 'dp'), may hold values from -0.0625 to 0.0625
- value_weight: bfloat16 [2, 4096, 1024], P('mp', 'dp'), may hold values from -0.0625 to 0.0625
- out_proj: bfloat16 [2, 8192, 8192], P('groups', 'mp', 'dp'), parts along dimension 0
Outputs:
- directions: float32 [160, 8192], P('groups', 'mp'), parts along dimension 0
- key_cache: bfloat16 [48, 128, 1024], P(('groups', 'dp'), None, 'mp'), parts along dimension 0
- value_cache: bfloat16 [48, 128, 1024], P(('groups', 'dp'), None, 'mp'), parts along dimension 0
- ortho_proj: bfloat16 [2, 8192, 8192], P('groups', 'mp', 'dp'), parts along dimension 0
There are 2 independent parts, one for each index of `groups`. A program takes and returns all parts, laid end to end along the dimension named above; an argument that names none is the same for every part. Nothing has to cross between parts.
Inputs may be any that keep to these rules, and one draw needn't show every extreme that they name: Every slab of 3 consecutive prompts holds both labels.
All inputs are finite; a program needn't handle non-finite values.
Results may differ from a plain program's by a relative error of at most 0.0051.
Values may be sent and summed in bfloat16 or wider, within the bound.
A program may use at most 384 MiB of HBM per device.

v0:
```python
import math

import jax
import jax.numpy as jnp
from jax import lax
from jax.sharding import PartitionSpec as P


def joined(value, axis, join):
    pieces = jax.tree.map(lambda part: lax.all_gather(part, axis), value)
    head = jax.tree.map(lambda part: part[0], pieces)
    tail = jax.tree.map(lambda part: part[1:], pieces)
    total, _ = lax.scan(lambda total, share: (join(total, share), None), head, tail)
    return total


def shards(
    residual, lengths, labels, earlier_means, chosen, norm_gain, key_weight, value_weight, out_proj
):
    highest = lax.Precision.HIGHEST
    prompts, length, half_width = residual.shape
    model_width = half_width * lax.axis_size("mp")
    positions = jnp.arange(length, dtype=jnp.int32)
    valid_mask = (positions[None, :] < lengths[:, None]).astype(jnp.bfloat16)
    masked_sums = jnp.einsum("pt,ptd->pd", valid_mask, residual, preferred_element_type=jnp.float32)
    prompt_mean = masked_sums / lengths.astype(jnp.float32)[:, None]
    onehot = (labels[:, None] == jnp.arange(2, dtype=jnp.int32)[None, :]).astype(jnp.float32)
    counts = jnp.sum(onehot, axis=0)
    current = jnp.dot(onehot.T, prompt_mean, precision=highest) / counts[:, None]
    layer_means = jnp.concatenate([earlier_means[0], current[None]], axis=0)

    def combine(left_pair, right_pair):
        joint_count = left_pair[0] + right_pair[0]
        blended = (
            left_pair[0][None, :, None] * left_pair[1]
            + right_pair[0][None, :, None] * right_pair[1]
        )
        return (joint_count, blended / joint_count[None, :, None])

    merged_counts, merged = joined((counts, layer_means), "dp", combine)
    difference = merged[:, 1] - merged[:, 0]
    square_sums = lax.psum(jnp.sum(difference * difference, axis=1), "mp")
    mean_dir = square_sums / model_width
    inverse_rms = lax.rsqrt(mean_dir + 1e-06)
    directions = difference * inverse_rms[:, None]
    chosen_layer = chosen[0]
    refusal_dir = lax.dynamic_index_in_dim(directions, chosen_layer, 0, keepdims=False) / math.sqrt(
        model_width
    )
    token_rows = residual.reshape(prompts * length, half_width)
    row_values = token_rows.astype(jnp.float32)
    projection_local = jnp.dot(row_values, refusal_dir, precision=highest)
    column_local = jnp.einsum(
        "r,ori->oi", refusal_dir, out_proj.astype(jnp.float32), precision=highest
    )
    projection, column_proj = lax.psum((projection_local, column_local), "mp")
    ablated = row_values - projection[:, None] * refusal_dir[None, :]
    mean_square = lax.psum(jnp.sum(ablated * ablated, axis=1), "mp") / model_width
    normed = (ablated * lax.rsqrt(mean_square + 1e-05)[:, None] * norm_gain[None, :]).astype(
        jnp.bfloat16
    )
    key_sum = jnp.dot(
        normed,
        lax.all_gather(key_weight, "dp", axis=1, tiled=True)[0],
        preferred_element_type=jnp.float32,
    )
    value_sum = jnp.dot(
        normed,
        lax.all_gather(value_weight, "dp", axis=1, tiled=True)[0],
        preferred_element_type=jnp.float32,
    )
    key_sums, value_sums = (
        lax.psum_scatter(key_sum, "mp", scatter_dimension=1, tiled=True),
        lax.psum_scatter(value_sum, "mp", scatter_dimension=1, tiled=True),
    )
    key_cache = key_sums.astype(jnp.bfloat16).reshape(prompts, length, key_sums.shape[1])
    value_cache = value_sums.astype(jnp.bfloat16).reshape(prompts, length, value_sums.shape[1])
    ortho_proj = (
        out_proj.astype(jnp.float32) - refusal_dir[None, :, None] * column_proj[:, None, :]
    ).astype(jnp.bfloat16)
    return (directions, key_cache, value_cache, ortho_proj)


def solution(mesh):
    return jax.shard_map(
        shards,
        mesh=mesh,
        in_specs=(
            P(("groups", "dp"), None, "mp"),
            P(("groups", "dp")),
            P(("groups", "dp")),
            P(("groups", "dp"), None, None, "mp"),
            P("groups"),
            P("mp"),
            P("mp", "dp", None),
            P("mp", "dp", None),
            P("groups", "mp", "dp"),
        ),
        out_specs=(
            P("groups", "mp"),
            P(("groups", "dp"), None, "mp"),
            P(("groups", "dp"), None, "mp"),
            P("groups", "mp", "dp"),
        ),
        check_vma=False,
    )
```

profile of v0, /device:TPU:24, one launch (start us, length us, event | category | flops | bytes accessed | tf_op | source)
XLA Modules:
  0.0 701.5 jit_solution(7702679912213129711)
XLA Ops:
  12.2 2.8 pad_maximum_fusion
  17.5 41.4 %all-reduce = f32[16]{0:T(128)S(1)} all-reduce(f32[16]{0:T(128)S(1)} %dynamic-update-slice), channel_id=2, replica_groups=mesh['groups'=2,'dp'=8,'mp'=2] {'dp'}, use_global_device_ids=true, to_apply=%add | all-reduce | flops 16 | bytes 128
  59.7 358.8 %all-gather.10.cloned.1.call-done = f32[640,2,4096]{2,1,0:T(2,128)} async-done(((f32[80,2,4096]{2,1,0:T(2,128)}), f32[640,2,4096]{2,1,0:T(2,128)}) %all-gather.10.cloned.1.call-update) | async-done | bytes 20971536 | tf_op jit(solution)/shard_map/all_gather | solution.py:10
  418.5 13.5 %slice.29 = f32[560,2,4096]{2,1,0:T(2,128)} slice(f32[640,2,4096]{2,1,0:T(2,128)} %all-gather.10.cloned.1.call-done), slice={[80:640], [0:2], [0:4096]} | slice | bytes 36700160 | tf_op jit(solution)/shard_map/slice | solution.py:12
  433.7 32.7 %while.12 = (s32[]{:T(128)}, f32[2]{0:T(128)S(1)}, f32[80,2,4096]{2,1,0:T(2,128)S(1)}, f32[7,2]{1,0:T(8,128)S(1)}, f32[7,80,2,4096]{3,2,1,0:T(2,128)}, /*index=5*/s32[]{:T(128)}) while((s32[]{:T(128)}, f32[2]{0:T(128)S(1)}, f32[80,2,4096]{2,1,0:T(2,128)S(1)}, f32[7,2]{1,0:T(8,128)S(1)}, f32[7,80,2,4096]{3,2,1,0:T(2,128)}, ...), condition=%wide.region_2.3_spmd, body=%wide.region_1.2_spmd.sunk | while | flops 2621444 | bytes 7864469 | solution.py:13
  433.7 4.6 fusion.27
  438.4 4.6 fusion.27
  443.1 4.6 fusion.27
  447.8 4.6 fusion.27
  452.4 4.6 fusion.27
  457.1 4.6 fusion.27
  461.8 4.6 fusion.27
  469.7 2.6 psum.28
  475.8 2.6 convolution_reduce_fusion
  478.4 2.7 psum.29
  482.2 5.7 fusion.3
  487.9 2.5 all-reduce.1
  490.4 3.4 multiply_convert_fusion
  493.7 50.0 %all-gather.6.cloned.1.call-done = bf16[1,4096,1024]{2,1,0:T(8,128)(2,1)} async-done(((bf16[1,512,1024]{2,1,0:T(8,128)(2,1)}), bf16[1,4096,1024]{2,1,0:T(8,128)(2,1)}) %all-gather.6.cloned.1.call-update) | async-done | bytes 8388624 | tf_op jit(solution)/shard_map/all_gather | solution.py:64
  543.7 9.0 %fusion.7 = f32[384,1024]{1,0:T(8,128)} fusion(bf16[384,4096]{1,0:T(8,128)(2,1)} %bitcast.63, bf16[1,4096,1024]{2,1,0:T(8,128)(2,1)} %all-gather.6.cloned.1.call-done), kind=kOutput, calls=%fused_computation.10 | convolution fusion | flops 3221225472 | bytes 13107200 | tf_op jit(solution)/shard_map/dot_general | solution.py:62
  552.8 116.2 %all-gather.8.cloned.1.call-done = bf16[1,4096,1024]{2,1,0:T(8,128)(2,1)} async-done(((bf16[1,512,1024]{2,1,0:T(8,128)(2,1)}), bf16[1,4096,1024]{2,1,0:T(8,128)(2,1)}) %all-gather.8.cloned.1.call-update) | async-done | bytes 8388624 | tf_op jit(solution)/shard_map/all_gather | solution.py:69
  669.0 6.9 fusion.5
  676.0 8.0 %subtract_convert_fusion = bf16[1,4096,1024]{2,1,0:T(8,128)(2,1)} fusion(bf16[1,4096,1024]{2,1,0:T(8,128)(2,1)} %param.19, f32[1024]{0:T(1024)S(1)} %get-tuple-element.43, f32[4096]{0:T(1024)S(1)} %bitcast.68), kind=kLoop, calls=%fused_computation.5 | loop fusion | flops 16777216 | bytes 16797696 | tf_op jit(solution)/shard_map/convert_element_type | solution.py:80
  685.9 7.2 %reduce-scatter.5.cloned.1.call-done = f32[384,512]{1,0:T(8,128)} async-done(((f32[384,1024]{1,0:T(8,128)}), f32[384,512]{1,0:T(8,128)}) %reduce-scatter.5.cloned.1.call-update) | async-done | bytes 786448 | tf_op jit(solution)/shard_map/reduce_scatter | solution.py:74
  (62 shorter events, 20.6 us)
Async XLA Ops:
  7.2 4.8 copy-start.6
  7.2 5.1 copy-start.3
  7.2 411.3 %all-gather.10.cloned.1.call-start = ((), (), s32[]{:S(2)}) async-start(), calls=%async_computation.6 | async-start | bytes 23592960 | tf_op jit(solution)/shard_map/all_gather | solution.py:10
  15.1 0.8 copy-start.7
  15.1 528.6 %all-gather.6.cloned.1.call-start = ((), (), s32[]{:S(2)}) async-start(), calls=%async_computation.2 | async-start | bytes 9437184 | tf_op jit(solution)/shard_map/all_gather | solution.py:64
  15.9 653.1 %all-gather.8.cloned.1.call-start = ((), (), s32[]{:S(2)}) async-start(), calls=%async_computation.4 | async-start | bytes 9437184 | tf_op jit(solution)/shard_map/all_gather | solution.py:69
  17.4 666.5 %reduce-scatter.3.cloned.1.call-start = ((), (), s32[]{:S(2)}) async-start(), calls=%async_computation.3 | async-start | bytes 2359296 | tf_op jit(solution)/shard_map/reduce_scatter | solution.py:73
  432.0 1.7 slice-start
  467.9 1.5 copy-start.1
  469.4 6.4 copy-start
  474.7 1.1 copy-start.4
  482.2 8.2 %copy-start.5 = (f32[4096]{0:T(1024)S(1)}, f32[4096]{0:T(1024)}, u32[]{:S(2)}) copy-start(f32[4096]{0:T(1024)} %param.16) | copy-start | bytes 49156
  543.7 125.3 %copy-start.2 = (bf16[3,128,4096]{2,1,0:T(8,128)(2,1)S(1)}, bf16[3,128,4096]{2,1,0:T(8,128)(2,1)}, u32[]{:S(2)}) copy-start(bf16[3,128,4096]{2,1,0:T(8,128)(2,1)} %multiply_convert_fusion) | copy-start | bytes 9437188
  552.8 140.3 %reduce-scatter.5.cloned.1.call-start = ((), (), s32[]{:S(2)}) async-start(), calls=%async_computation.5 | async-start | bytes 2359296 | tf_op jit(solution)/shard_map/reduce_scatter | solution.py:74
Sparse Core Ops, SparseCore 0:
  15.2 403.2 all-gather.9
  420.6 123.0 all-gather.5
  545.9 123.1 all-gather.7
  671.1 9.4 reduce-scatter.2
  682.8 10.2 reduce-scatter.4
where the time goes:
time: 704 us; the launch traced here: 702 us
  waiting for transfers between devices  533 us (76%)
  other arithmetic  56.7 us (8%)
  blocking collectives  49.2 us (7%)
  matrix products  26.9 us (4%)
  local copies, waits for them, and re-layouts  20.3 us (3%)
  between operations  15.2 us (2%)
    all_gather x1, waiting for transfers between devices, joined(): pieces = jax.tree.map(lambda part: lax.all_gather(part, axis), value)  359 us
    all_gather x1, waiting for transfers between devices, shards(): lax.all_gather(value_weight, 'dp', axis=1, tiled=True)[0]  116 us
    all_gather x1, waiting for transfers between devices, shards(): lax.all_gather(key_weight, 'dp', axis=1, tiled=True)[0]  50 us
    unnamed x1, blocking collectives  41.4 us
    div x7, other arithmetic, combine(): return (joint_count, blended / joint_count[None, :, None])  32.4 us
  transfers between devices with their start and end apart: 5, of which 4 were waited for; matrix products, arithmetic and copies ran while one was open for 13% of the time, Pallas kernels for 0%

commit v1 on v0

v1 whole, which is shorter than its diff:
```python
import math

import jax
import jax.numpy as jnp
from jax import lax
from jax.sharding import PartitionSpec as P


def direction_parts(residual, lengths, labels, earlier_means, chosen):
    highest = lax.Precision.HIGHEST
    length = residual.shape[1]
    positions = jnp.arange(length, dtype=jnp.int32)
    valid_mask = (positions[None, :] < lengths[:, None]).astype(jnp.bfloat16)
    masked_sums = jnp.einsum("pt,ptd->pd", valid_mask, residual, preferred_element_type=jnp.float32)
    prompt_mean = masked_sums / lengths.astype(jnp.float32)[:, None]
    onehot = (labels[:, None] == jnp.arange(2, dtype=jnp.int32)[None, :]).astype(jnp.float32)
    counts = jnp.sum(onehot, axis=0)
    current = jnp.sum(onehot[:, :, None] * prompt_mean[:, None, :], axis=0) / counts[:, None]
    earlier = earlier_means[0]
    layers = earlier.shape[0] + 1
    picked = lax.dynamic_index_in_dim(
        earlier, jnp.minimum(chosen[0], layers - 2), 0, keepdims=False
    )
    picked = jnp.where(chosen[0] == layers - 1, current, picked)
    weighted, totals = lax.psum((counts[:, None] * picked, counts), "dp")
    merged = weighted / totals[:, None]
    picked_difference = merged[1] - merged[0]
    share = counts / totals
    local = jnp.concatenate(
        [
            share[1] * earlier[:, 1] - share[0] * earlier[:, 0],
            (share[1] * current[1] - share[0] * current[0])[None],
        ],
        axis=0,
    )
    return picked_difference, local


def shards(
    residual, lengths, labels, earlier_means, chosen, norm_gain, key_weight, value_weight, out_proj
):
    highest = lax.Precision.HIGHEST
    prompts, length, half_width = residual.shape
    model_width = half_width * lax.axis_size("mp")
    picked_difference, local = direction_parts(residual, lengths, labels, earlier_means, chosen)

    key_full = lax.all_gather(key_weight, "dp", axis=1, tiled=True)[0]
    value_full = lax.all_gather(value_weight, "dp", axis=1, tiled=True)[0]

    difference = lax.psum(local, "dp")
    square_sums = lax.psum(jnp.sum(difference * difference, axis=1), "mp")
    directions = difference * lax.rsqrt(square_sums / model_width + 1e-06)[:, None]

    local_square = jnp.sum(picked_difference * picked_difference)
    local_mean = local_square / half_width + 1e-06
    unit = picked_difference * lax.rsqrt(local_mean)
    token_rows = residual.reshape(prompts * length, half_width)
    row_values = token_rows.astype(jnp.float32)
    matrix = out_proj[0]
    dots = jnp.sum(row_values * unit[None, :], axis=1)
    columns = jnp.sum(matrix.astype(jnp.float32) * unit[:, None], axis=0)
    packed = jnp.concatenate([dots, columns, local_square[None]])
    pieces = lax.all_gather(packed, "mp")
    squares = pieces[:, -1]
    mean_dir = jnp.sum(squares) / model_width + 1e-06
    ratios = jnp.sqrt((squares / half_width + 1e-06) / mean_dir) / math.sqrt(model_width)
    sums = jnp.sum(pieces * ratios[:, None], axis=0)
    projection = sums[: prompts * length]
    column_proj = sums[prompts * length : -1]
    refusal_dir = picked_difference * (lax.rsqrt(mean_dir) / math.sqrt(model_width))

    ablated = row_values - projection[:, None] * refusal_dir[None, :]
    mean_square = lax.psum(jnp.sum(ablated * ablated, axis=1), "mp") / model_width
    normed = (ablated * lax.rsqrt(mean_square + 1e-05)[:, None] * norm_gain[None, :]).astype(
        jnp.bfloat16
    )
    ortho_proj = (matrix.astype(jnp.float32) - refusal_dir[:, None] * column_proj[None, :]).astype(
        jnp.bfloat16
    )[None]
    key_sum = jnp.dot(normed, key_full, preferred_element_type=jnp.float32)
    value_sum = jnp.dot(normed, value_full, preferred_element_type=jnp.float32)
    key_sums, value_sums = (
        lax.psum_scatter(key_sum, "mp", scatter_dimension=1, tiled=True),
        lax.psum_scatter(value_sum, "mp", scatter_dimension=1, tiled=True),
    )
    key_cache = key_sums.astype(jnp.bfloat16).reshape(prompts, length, key_sums.shape[1])
    value_cache = value_sums.astype(jnp.bfloat16).reshape(prompts, length, value_sums.shape[1])
    return (directions, key_cache, value_cache, ortho_proj)


def solution(mesh):
    return jax.shard_map(
        shards,
        mesh=mesh,
        in_specs=(
            P(("groups", "dp"), None, "mp"),
            P(("groups", "dp")),
            P(("groups", "dp")),
            P(("groups", "dp"), None, None, "mp"),
            P("groups"),
            P("mp"),
            P("mp", "dp", None),
            P("mp", "dp", None),
            P("groups", "mp", "dp"),
        ),
        out_specs=(
            P("groups", "mp"),
            P(("groups", "dp"), None, "mp"),
            P(("groups", "dp"), None, "mp"),
            P("groups", "mp", "dp"),
        ),
        check_vma=False,
    )
```

time: 704 us -> 426 us (0.61)
  waiting for transfers between devices: 533 us -> 307 us
  other arithmetic: 56.7 us -> 37.5 us
  local copies, waits for them, and re-layouts: 20.3 us -> 6.11 us
  matrix products: 26.9 us -> 16.6 us
  blocking collectives: 49.2 us -> 40.4 us
    all_gather x3 -> x2, waiting for transfers between devices: 525 us -> 235 us  [the longest x1 119 us: shards(): key_full = lax.all_gather(key_weight, 'dp', axis=1, tiled=True)[0]]
    psum x0 -> x1, waiting for transfers between devices: none -> 64.4 us  [shards(): difference = lax.psum(local, 'dp')]
    unnamed x1, blocking collectives: 41.4 us -> 3.28 us
    div x8 -> x4, other arithmetic: 32.4 us -> 0.29 us  [the longest x1 0.12 us: shards(): jnp.sqrt((squares / half_width + 1e-06) / mean_dir) / math.sqrt(model_width)]
    psum x2 -> x1, blocking collectives: 5.12 us -> 34.7 us  [direction_parts(): weighted, totals = lax.psum((counts[:, None] * picked, counts), 'dp')]
    slice x5 -> x2, local copies, waits for them, and re-layouts: 15.4 us -> 0.59 us  [the longest x1 0.59 us: direction_parts(): share[1] * earlier[:, 1] - share[0] * earlier[:, 0]]
    dot_general x6 -> x3, matrix products: 26.9 us -> 16.6 us  [the longest x1 9.04 us: shards(): key_sum = jnp.dot(normed, key_full, preferred_element_type=jnp.float32)]
    reduce_sum x1 -> x7, other arithmetic: 0.77 us -> 8.32 us  [the longest x1 5.4 us: shards(): columns = jnp.sum(matrix.astype(jnp.float32) * unit[:, None], axis=0)]
  transfers between devices with their start and end apart: 5 -> 5, of which waited for: 4 -> 4; matrix products, arithmetic and copies ran while one was open for 13% -> 10% of each run, Pallas kernels for 0% -> 0%
where the time goes in v1:
time: 426 us; the launch traced here: 424 us
  waiting for transfers between devices  307 us (72%)
  blocking collectives  40.4 us (9%)
  other arithmetic  37.5 us (9%)
  matrix products  16.6 us (4%)
  between operations  16.6 us (4%)
  local copies, waits for them, and re-layouts  6.11 us (1%)
    all_gather x1, waiting for transfers between devices, shards(): key_full = lax.all_gather(key_weight, 'dp', axis=1, tiled=True)[0]  119 us
    all_gather x1, waiting for transfers between devices, shards(): value_full = lax.all_gather(value_weight, 'dp', axis=1, tiled=True)[0]  116 us
    psum x1, waiting for transfers between devices, shards(): difference = lax.psum(local, 'dp')  64.4 us
    psum x1, blocking collectives, direction_parts(): weighted, totals = lax.psum((counts[:, None] * picked, counts), 'dp')  34.7 us
    dot_general x1, matrix products, shards(): key_sum = jnp.dot(normed, key_full, preferred_element_type=jnp.float32)  9.04 us
  transfers between devices with their start and end apart: 5, of which 4 were waited for; matrix products, arithmetic and copies ran while one was open for 10% of the time, Pallas kernels for 0%

profile of v1, /device:TPU:24, one launch (start us, length us, event | category | flops | bytes accessed | tf_op | source)
XLA Modules:
  0.0 424.3 jit_solution(17136357276199874435)
XLA Ops:
  7.2 0.9 fusion.14
  11.0 4.7 %copy.24 = f32[1,79,2,4096]{3,1,2,0:T(8,128)} copy(f32[1,79,2,4096]{3,2,1,0:T(2,128)} %param.12) | data formatting | bytes 5177344 | tf_op args[3]
  16.4 0.9 fusion.10
  17.3 34.7 %all-reduce.1 = (f32[2]{0:T(128)S(1)}, f32[2,4096]{1,0:T(2,128)S(1)}) all-reduce(f32[2]{0:T(128)S(1)} %fusion.15, f32[2,4096]{1,0:T(2,128)S(1)} %get-tuple-element.10), channel_id=1, replica_groups=mesh['groups'=2,'dp'=8,'mp'=2] {'dp'}, use_global_device_ids=true, to_apply=%region_1.0 | all-reduce | flops 8194 | bytes 65552 | tf_op jit(solution)/shard_map/psum | solution.py:25
  52.6 1.3 fusion.11
  53.9 3.1 fusion.9
  57.0 1.2 pad_maximum_fusion
  63.2 5.4 %fusion.1 = f32[1024]{0:T(1024)S(1)} fusion(bf16[1,4096,1024]{2,1,0:T(8,128)(2,1)} %param.17, f32[4096]{0:T(1024)S(1)} %bitcast.54), kind=kLoop, calls=%fused_computation.3 | loop fusion | flops 12581888 | bytes 8409088 | tf_op jit(solution)/shard_map/reduce_sum | solution.py:61
  68.6 0.8 maximum_dynamic-update-slice_fusion
  69.4 3.3 all-reduce
  74.3 1.2 multiply_reduce_fusion
  75.5 64.4 %all-reduce.5.cloned.1.call-done = f32[80,4096]{1,0:T(8,128)} async-done(((f32[80,4096]{1,0:T(8,128)}), f32[80,4096]{1,0:T(8,128)}) %all-reduce.5.cloned.1.call-update) | async-done | bytes 1310736 | tf_op jit(solution)/shard_map/psum | solution.py:50
  139.8 1.5 multiply_reduce_fusion.1
  141.3 2.5 all-reduce.2
  143.8 3.4 multiply_convert_fusion
  147.2 119.0 %all-gather.4.cloned.1.call-done = bf16[1,4096,1024]{2,1,0:T(8,128)(2,1)} async-done(((bf16[1,512,1024]{2,1,0:T(8,128)(2,1)}), bf16[1,4096,1024]{2,1,0:T(8,128)(2,1)}) %all-gather.4.cloned.1.call-update) | async-done | bytes 8388624 | tf_op jit(solution)/shard_map/all_gather | solution.py:47
  266.2 9.0 %fusion.5 = f32[384,1024]{1,0:T(8,128)} fusion(bf16[384,4096]{1,0:T(8,128)(2,1)} %bitcast.46, bf16[1,4096,1024]{2,1,0:T(8,128)(2,1)} %all-gather.4.cloned.1.call-done), kind=kOutput, calls=%fused_computation.7 | convolution fusion | flops 3221225472 | bytes 13107200 | tf_op jit(solution)/shard_map/dot_general | solution.py:80
  275.3 116.4 %all-gather.6.cloned.1.call-done = bf16[1,4096,1024]{2,1,0:T(8,128)(2,1)} async-done(((bf16[1,512,1024]{2,1,0:T(8,128)(2,1)}), bf16[1,4096,1024]{2,1,0:T(8,128)(2,1)}) %all-gather.6.cloned.1.call-update) | async-done | bytes 8388624 | tf_op jit(solution)/shard_map/all_gather | solution.py:48
  391.7 7.0 %fusion.3 = f32[384,1024]{1,0:T(8,128)} fusion(bf16[384,4096]{1,0:T(8,128)(2,1)S(1)} %bitcast.47, bf16[1,4096,1024]{2,1,0:T(8,128)(2,1)} %all-gather.6.cloned.1.call-done), kind=kOutput, calls=%fused_computation.5 | convolution fusion | flops 3221225472 | bytes 13107200 | tf_op jit(solution)/shard_map/dot_general | solution.py:81
  398.8 8.2 %fusion.2 = bf16[1,4096,1024]{2,1,0:T(8,128)(2,1)} fusion(bf16[1,4096,1024]{2,1,0:T(8,128)(2,1)} %param.17, f32[1024]{0:T(1024)S(1)} %slice.54, f32[4096]{0:T(1024)S(1)} %bitcast.52), kind=kLoop, calls=%fused_computation.4 | loop fusion | flops 16777216 | bytes 16797696 | tf_op jit(solution)/shard_map/convert_element_type | solution.py:77
  407.0 1.2 broadcast_multiply_fusion
  408.2 1.9 convert_element_type.52
  410.2 5.7 %reduce-scatter.5.cloned.1.call-done = f32[384,512]{1,0:T(8,128)} async-done(((f32[384,1024]{1,0:T(8,128)}), f32[384,512]{1,0:T(8,128)}) %reduce-scatter.5.cloned.1.call-update) | async-done | bytes 786448 | tf_op jit(solution)/shard_map/reduce_scatter | solution.py:84
  415.8 1.9 convert_element_type.53
  (45 shorter events, 8.1 us)
Async XLA Ops:
  7.2 8.5 %copy-start = (bf16[3,128,4096]{2,1,0:T(8,128)(2,1)S(1)}, bf16[3,128,4096]{2,1,0:T(8,128)(2,1)}, u32[]{:S(2)}) copy-start(bf16[3,128,4096]{2,1,0:T(8,128)(2,1)} %param.9) | copy-start | bytes 9437188
  7.2 132.7 %all-reduce.5.cloned.1.call-start = ((), (), s32[]{:S(2)}) async-start(), calls=%async_computation.2 | async-start | bytes 2621440 | tf_op jit(solution)/shard_map/psum | solution.py:50
  57.0 4.2 copy-start.4
  58.2 208.0 %all-gather.4.cloned.1.call-start = ((), (), s32[]{:S(2)}) async-start(), calls=%async_computation.3 | async-start | bytes 9437184 | tf_op jit(solution)/shard_map/all_gather | solution.py:47
  59.0 332.8 %all-gather.6.cloned.1.call-start = ((), (), s32[]{:S(2)}) async-start(), calls=%async_computation.5 | async-start | bytes 9437184 | tf_op jit(solution)/shard_map/all_gather | solution.py:48
  59.7 348.5 %reduce-scatter.3.cloned.1.call-start = ((), (), s32[]{:S(2)}) async-start(), calls=%async_computation.4 | async-start | bytes 2359296 | tf_op jit(solution)/shard_map/reduce_scatter | solution.py:83
  68.6 75.2 %copy-start.3 = (f32[4096]{0:T(1024)S(1)}, f32[4096]{0:T(1024)}, u32[]{:S(2)}) copy-start(f32[4096]{0:T(1024)} %param.14) | copy-start | bytes 49156
  266.2 125.5 %copy-start.2 = (bf16[3,128,4096]{2,1,0:T(8,128)(2,1)S(1)}, bf16[3,128,4096]{2,1,0:T(8,128)(2,1)}, u32[]{:S(2)}) copy-start(bf16[3,128,4096]{2,1,0:T(8,128)(2,1)} %multiply_convert_fusion) | copy-start | bytes 9437188
  275.3 140.5 %reduce-scatter.5.cloned.1.call-start = ((), (), s32[]{:S(2)}) async-start(), calls=%async_computation.6 | async-start | bytes 2359296 | tf_op jit(solution)/shard_map/reduce_scatter | solution.py:84
  398.8 8.2 %copy-start.1 = (f32[80,4096]{1,0:T(8,128)S(1)}, f32[80,4096]{1,0:T(8,128)}, u32[]{:S(2)}) copy-start(f32[80,4096]{1,0:T(8,128)} %all-reduce.5.cloned.1.call-done) | copy-start | bytes 3932164
Sparse Core Ops, SparseCore 0:
  58.4 81.4 all-reduce.4
  142.2 124.0 all-gather.3
  268.6 123.1 all-gather.5
  393.9 9.4 reduce-scatter.2
  405.5 10.2 reduce-scatter.4

commit v2 on v1

--- a/solution.py
+++ b/solution.py
@@ -36,25 +36,91 @@
     return picked_difference, local
 
 
+def pair_perm(axis_size):
+    return [(i, i ^ 1) for i in range(axis_size)]
+
+
+def chain_pieces(own, groups, width, parts):
+    lines = width // 2
+    axes = ("groups", "dp")
+    rows = own.shape[0] // parts
+    place = lax.axis_index("dp") // 2
+
+    def hop(value, step, way):
+        pairs = []
+        for g in range(groups):
+            for j in range(width):
+                z = j // 2
+                if way > 0 and step - 1 <= z < lines - 1:
+                    pairs.append((g * width + j, g * width + j + 2))
+                if way < 0 and 0 < z <= lines - step:
+                    pairs.append((g * width + j, g * width + j - 2))
+        return lax.ppermute(value, axes, pairs)
+
+    def cross(value, step, way):
+        pairs = []
+        for g in range(groups):
+            for j in range(width):
+                z = j // 2
+                if (way > 0 and z >= step) or (way < 0 and z < lines - step):
+                    pairs.append((g * width + j, (g ^ 1) * width + j))
+        return lax.ppermute(value, axes, pairs)
+
+    chain = {}
+    crossed = {}
+    for way in (1, -1):
+        for part in range(parts):
+            chain[way, 0, part] = own[part * rows : (part + 1) * rows]
+    for step in range(1, lines):
+        for part in range(parts):
+            for way in (1, -1):
+                chain[way, step, part] = hop(chain[way, step - 1, part], step, way)
+                crossed[way, step, part] = cross(chain[way, step, part], step, way)
+
+    def merged(table):
+        blocks = []
+        for step in range(1, lines):
+            for part in range(parts):
+                blocks.append(
+                    jnp.where(place >= step, table[1, step, part], table[-1, lines - step, part])
+                )
+        return blocks
+
+    return merged(chain), merged(crossed)
+
+
 def shards(
     residual, lengths, labels, earlier_means, chosen, norm_gain, key_weight, value_weight, out_proj
 ):
-    highest = lax.Precision.HIGHEST
     prompts, length, half_width = residual.shape
+    tokens = prompts * length
     model_width = half_width * lax.axis_size("mp")
+    groups, width = lax.axis_size("groups"), lax.axis_size("dp")
+    lines = width // 2
+    block = half_width // width
+    even = lax.axis_index("groups") % 2 == 0
+    place = lax.axis_index("dp") // 2
+    side = lax.axis_index("dp") % 2
+    core = lax.axis_index("mp")
+
+    token_rows = residual.reshape(tokens, half_width)
+    blocked = token_rows.reshape(tokens, lines, 2 * block)
+    wanted = lax.dynamic_slice_in_dim(blocked, (1 - side) * block, block, 2)
+    neighbour_rows = lax.ppermute(wanted.reshape(tokens, lines * block), "dp", pair_perm(width))
+    key_own, value_own = key_weight[0], value_weight[0]
+    chain_own = jnp.where(even, key_own, value_own)
+    cross_own = jnp.where(even, value_own, key_own)
+    chain, crossed = chain_pieces(chain_own, groups, width, 2)
+
     picked_difference, local = direction_parts(residual, lengths, labels, earlier_means, chosen)
-
-    key_full = lax.all_gather(key_weight, "dp", axis=1, tiled=True)[0]
-    value_full = lax.all_gather(value_weight, "dp", axis=1, tiled=True)[0]
-
     difference = lax.psum(local, "dp")
-    square_sums = lax.psum(jnp.sum(difference * difference, axis=1), "mp")
+    square_half = jnp.sum(difference * difference, axis=1)
+    square_sums = square_half + lax.ppermute(square_half, "mp", pair_perm(2))
     directions = difference * lax.rsqrt(square_sums / model_width + 1e-06)[:, None]
 
     local_square = jnp.sum(picked_difference * picked_difference)
     local_mean = local_square / half_width + 1e-06
     unit = picked_difference * lax.rsqrt(local_mean)
-    token_rows = residual.reshape(prompts * length, half_width)
     row_values = token_rows.astype(jnp.float32)
     matrix = out_proj[0]
     dots = jnp.sum(row_values * unit[None, :], axis=1)
@@ -65,26 +131,52 @@
     mean_dir = jnp.sum(squares) / model_width + 1e-06
     ratios = jnp.sqrt((squares / half_width + 1e-06) / mean_dir) / math.sqrt(model_width)
     sums = jnp.sum(pieces * ratios[:, None], axis=0)
-    projection = sums[: prompts * length]
-    column_proj = sums[prompts * length : -1]
+    projection = sums[:tokens]
+    column_proj = sums[tokens:-1]
     refusal_dir = picked_difference * (lax.rsqrt(mean_dir) / math.sqrt(model_width))
 
     ablated = row_values - projection[:, None] * refusal_dir[None, :]
     mean_square = lax.psum(jnp.sum(ablated * ablated, axis=1), "mp") / model_width
-    normed = (ablated * lax.rsqrt(mean_square + 1e-05)[:, None] * norm_gain[None, :]).astype(
-        jnp.bfloat16
-    )
+    scale = lax.rsqrt(mean_square + 1e-05)
     ortho_proj = (matrix.astype(jnp.float32) - refusal_dir[:, None] * column_proj[None, :]).astype(
         jnp.bfloat16
     )[None]
-    key_sum = jnp.dot(normed, key_full, preferred_element_type=jnp.float32)
-    value_sum = jnp.dot(normed, value_full, preferred_element_type=jnp.float32)
-    key_sums, value_sums = (
-        lax.psum_scatter(key_sum, "mp", scatter_dimension=1, tiled=True),
-        lax.psum_scatter(value_sum, "mp", scatter_dimension=1, tiled=True),
-    )
-    key_cache = key_sums.astype(jnp.bfloat16).reshape(prompts, length, key_sums.shape[1])
-    value_cache = value_sums.astype(jnp.bfloat16).reshape(prompts, length, value_sums.shape[1])
+
+    stats = jnp.stack([projection, scale])
+    both = jnp.concatenate([stats, lax.ppermute(stats, "dp", pair_perm(width))], axis=1)
+    mine = lax.dynamic_slice_in_dim(blocked, side * block, block, 2).reshape(tokens, lines * block)
+
+    def feature_part(vector):
+        return lax.dynamic_slice_in_dim(vector.reshape(lines, 2 * block), side * block, block, 1)
+
+    rows = jnp.concatenate([mine, neighbour_rows], axis=0).astype(jnp.float32)
+    normed = (
+        (rows - both[0][:, None] * feature_part(refusal_dir).reshape(1, -1))
+        * both[1][:, None]
+        * feature_part(norm_gain).reshape(1, -1)
+    ).astype(jnp.bfloat16)
+    ordered = jnp.concatenate(
+        [
+            lax.dynamic_slice_in_dim(normed, (place - step + lines) % lines * block, block, 1)
+            for step in range(lines)
+        ],
+        axis=1,
+    )
+
+    def finish(own, blocks):
+        weight = jnp.concatenate([own] + blocks, axis=0)
+        total = jnp.dot(ordered, weight, preferred_element_type=jnp.float32)
+        half = total.shape[1] // 2
+        away = lax.dynamic_slice_in_dim(total, (1 - core) * half, half, 1)
+        kept = lax.dynamic_slice_in_dim(total, core * half, half, 1)
+        kept = kept + lax.ppermute(away, "mp", pair_perm(2))
+        result = kept[:tokens] + lax.ppermute(kept[tokens:], "dp", pair_perm(width))
+        return result.astype(jnp.bfloat16).reshape(prompts, length, half)
+
+    chain_out = finish(chain_own, chain)
+    cross_out = finish(cross_own, crossed)
+    key_cache = jnp.where(even, chain_out, cross_out)
+    value_cache = jnp.where(even, cross_out, chain_out)
     return (directions, key_cache, value_cache, ortho_proj)
 
 

time: 426 us -> 318 us (0.75)
  waiting for transfers between devices: 307 us -> 129 us
  starting transfers between devices: 0.2 us -> 49.8 us
  local copies, waits for them, and re-layouts: 6.11 us -> 23.5 us
  other arithmetic: 37.5 us -> 46.8 us
  matrix products: 16.6 us -> 7.32 us
    all_gather x2 -> x0, waiting for transfers between devices: 235 us -> none  [the longest x1 119 us: shards(): key_full = lax.all_gather(key_weight, 'dp', axis=1, tiled=True)[0]]
    ppermute x0 -> x31, waiting for transfers between devices: none -> 79.4 us  [the longest x12 31.7 us: cross(): return lax.ppermute(value, axes, pairs)]
    ppermute x0 -> x31, starting transfers between devices: none -> 49.7 us  [the longest x12 22.8 us: cross(): return lax.ppermute(value, axes, pairs)]
    psum x1, waiting for transfers between devices: 64.4 us -> 49.3 us  [shards(): difference = lax.psum(local, 'dp')]
    unnamed x1 -> x13, other arithmetic: 0.77 us -> 14.4 us
    dot_general x2, matrix products: 16.1 us -> 6.81 us  [finish(): total = jnp.dot(ordered, weight, preferred_element_type=jnp.float32)]
    dynamic_slice x0 -> x4, local copies, waits for them, and re-layouts: none -> 6.09 us  [the longest x1 3.05 us: shards(): lax.dynamic_slice_in_dim(blocked, side * block, block, 2)]
    reduce_scatter x2 -> x0, waiting for transfers between devices: 5.67 us -> none  [the longest x1 5.66 us: shards(): lax.psum_scatter(value_sum, 'mp', scatter_dimension=1, tiled=True)]
  transfers between devices with their start and end apart: 5 -> 32, of which waited for: 4 -> 9; matrix products, arithmetic and copies ran while one was open for 10% -> 21% of each run, Pallas kernels for 0% -> 0%
where the time goes in v2:
time: 318 us; the launch traced here: 317 us
  waiting for transfers between devices  129 us (41%)
  starting transfers between devices  49.8 us (16%)
  other arithmetic  46.8 us (15%)
  blocking collectives  43.3 us (14%)
  local copies, waits for them, and re-layouts  23.5 us (7%)
  between operations  17.6 us (6%)
  matrix products  7.32 us (2%)
    psum x1, waiting for transfers between devices, shards(): difference = lax.psum(local, 'dp')  49.3 us
    psum x1, blocking collectives, direction_parts(): weighted, totals = lax.psum((counts[:, None] * picked, counts), 'dp')  37.5 us
    ppermute x12, waiting for transfers between devices, cross(): return lax.ppermute(value, axes, pairs)  31.7 us
    ppermute x2, waiting for transfers between devices, finish(): result = kept[:tokens] + lax.ppermute(kept[tokens:], 'dp', pair_perm(width))  31.6 us
    ppermute x12, starting transfers between devices, cross(): return lax.ppermute(value, axes, pairs)  22.8 us
    ppermute x12, starting transfers between devices, hop(): return lax.ppermute(value, axes, pairs)  22.5 us
    ppermute x12, waiting for transfers between devices, hop(): return lax.ppermute(value, axes, pairs)  16.1 us
    unnamed x13, other arithmetic  14.4 us
  transfers between devices with their start and end apart: 32, of which 9 were waited for; matrix products, arithmetic and copies ran while one was open for 21% of the time, Pallas kernels for 0%

profile of v2, /device:TPU:24, one launch (start us, length us, event | category | flops | bytes accessed | tf_op | source)
XLA Modules:
  0.0 316.9 jit_solution(18272805580885435751)
XLA Ops:
  7.2 3.4 %bitcast_dynamic-update-slice_fusion.1 = (bf16[2048,1024]{1,0:T(8,128)(2,1)}, bf16[1,512,1024]{2,1,0:T(8,128)(2,1)S(1)}, bf16[2048,1024]{1,0:T(8,128)(2,1)}) fusion(bf16[1,512,1024]{2,1,0:T(8,128)(2,1)} %param.15, bf16[1,512,1024]{2,1,0:T(8,128)(2,1)} %param.16, pred[]{:T(512)S(6)} %eq.36), kind=kLoop, calls=%fused_computation.22 | loop fusion | flops 1048574 | bytes 5242881
  11.8 3.3 %collective-permute-start.4 = (bf16[256,1024]{1,0:T(8,128)(2,1)}, bf16[256,1024]{1,0:T(8,128)(2,1)}, u32[]{:S(2)}, u32[]{:S(2)}) collective-permute-start(bf16[256,1024]{1,0:T(8,128)(2,1)} %get-tuple-element.27), channel_id=1, source_target_pairs={{4,0},{6,2},{8,4},{10,6},{12,8},{14,10},{20,16},{22,18},{24,20},{2... | collective-permute-start | bytes 1572872 | tf_op jit(solution)/shard_map/ppermute | solution.py:58
  16.3 5.4 %collective-permute-start.8 = (bf16[256,1024]{1,0:T(8,128)(2,1)}, bf16[256,1024]{1,0:T(8,128)(2,1)}, u32[]{:S(2)}, u32[]{:S(2)}) collective-permute-start(bf16[256,1024]{1,0:T(8,128)(2,1)} %get-tuple-element.26), channel_id=1, source_target_pairs={{4,0},{6,2},{8,4},{10,6},{12,8},{14,10},{20,16},{22,18},{24,20},{2... | collective-permute-start | bytes 1572872 | tf_op jit(solution)/shard_map/ppermute | solution.py:58
  24.0 4.8 %copy.28 = f32[1,79,2,4096]{3,1,2,0:T(8,128)} copy(f32[1,79,2,4096]{3,2,1,0:T(2,128)} %param.12) | data formatting | bytes 5177344 | tf_op args[3]
  30.3 37.5 %all-reduce.1 = (f32[2]{0:T(128)S(1)}, f32[2,4096]{1,0:T(2,128)S(1)}) all-reduce(f32[2]{0:T(128)S(1)} %fusion.19, f32[2,4096]{1,0:T(2,128)S(1)} %get-tuple-element.17), channel_id=1, replica_groups=mesh['groups'=2,'dp'=8,'mp'=2] {'dp'}, use_global_device_ids=true, to_apply=%region_1.2 | all-reduce | flops 8194 | bytes 65552 | tf_op jit(solution)/shard_map/psum | solution.py:25
  76.3 5.1 %fusion.1 = f32[1024]{0:T(1024)S(1)} fusion(bf16[1,4096,1024]{2,1,0:T(8,128)(2,1)} %param.17, f32[4096]{0:T(1024)S(1)} %bitcast.64), kind=kLoop, calls=%fused_computation.3 | loop fusion | flops 12581888 | bytes 8409088 | tf_op jit(solution)/shard_map/reduce_sum | solution.py:127
  83.4 3.3 %all-reduce = f32[2818]{0:T(1024)S(1)} all-reduce(f32[2818]{0:T(1024)S(1)} %maximum_dynamic-update-slice_fusion), channel_id=2, replica_groups=mesh['groups'=2,'dp'=8,'mp'=2] {'mp'}, use_global_device_ids=true, to_apply=%add | all-reduce | flops 2818 | bytes 22544
  97.1 4.0 %reshape_reshape.3 = bf16[384,4,1024]{2,1,0:T(4,128)(2,1)} reshape(bf16[3,128,4096]{2,1,0:T(8,128)(2,1)S(1)} %copy-done) | data formatting | bytes 6291456 | tf_op jit(solution)/shard_map/reshape;reshape | solution.py:107
  113.3 49.3 %all-reduce.4.cloned.1.call-done = f32[80,4096]{1,0:T(8,128)} async-done(((f32[80,4096]{1,0:T(8,128)}), f32[80,4096]{1,0:T(8,128)}) %all-reduce.4.cloned.1.call-update) | async-done | bytes 1310736 | tf_op jit(solution)/shard_map/psum | solution.py:116
  164.1 3.4 %collective-permute-start.17 = (bf16[256,1024]{1,0:T(8,128)(2,1)}, bf16[256,1024]{1,0:T(8,128)(2,1)S(1)}, u32[]{:S(2)}, u32[]{:S(2)}) collective-permute-start(bf16[256,1024]{1,0:T(8,128)(2,1)} %collective-permute-done.3), channel_id=1, source_target_pairs={{4,20},{6,22},{8,24},{10,26},{12,28},{14,30},{20,4},{22,6},{24,8},... | collective-permute-start | bytes 1572872 | tf_op jit(solution)/shard_map/ppermute | solution.py:67
  180.8 8.2 %collective-permute-done.13 = bf16[256,1024]{1,0:T(8,128)(2,1)S(1)} collective-permute-done((bf16[256,1024]{1,0:T(8,128)(2,1)}, bf16[256,1024]{1,0:T(8,128)(2,1)S(1)}, u32[]{:S(2)}, u32[]{:S(2)}) %collective-permute-start.13) | collective-permute-done | bytes 524320 | tf_op jit(solution)/shard_map/ppermute | solution.py:58
  190.7 7.8 %collective-permute-done.14 = bf16[256,1024]{1,0:T(8,128)(2,1)S(1)} collective-permute-done((bf16[256,1024]{1,0:T(8,128)(2,1)}, bf16[256,1024]{1,0:T(8,128)(2,1)S(1)}, u32[]{:S(2)}, u32[]{:S(2)}) %collective-permute-start.14) | collective-permute-done | bytes 524320 | tf_op jit(solution)/shard_map/ppermute | solution.py:58
  205.4 3.4 %fusion.11 = f32[768,1024]{1,0:T(8,128)S(1)} fusion(bf16[2048,1024]{1,0:T(8,128)(2,1)S(1)} %copy-done.5, bf16[768,512]{1,0:T(8,128)(2,1)S(1)} %get-tuple-element.20, bf16[768,512]{1,0:T(8,128)(2,1)S(1)} %get-tuple-element.21, bf16[768,512]{1,0:T(8,128)(2,1)S(1)} %get-tuple-element.22, bf16[768,512]{1,0:T(8,128)(2,1)S(1)} %get-tuple-element.19), kind=kOutput, calls=%fused_computation.30 | convolution fusion | flops 3233808384 | bytes 10485760 | tf_op jit(solution)/shard_map/dot_general | solution.py:168
  210.2 3.4 %collective-permute-start.21 = (bf16[256,1024]{1,0:T(8,128)(2,1)}, bf16[256,1024]{1,0:T(8,128)(2,1)S(1)}, u32[]{:S(2)}, u32[]{:S(2)}) collective-permute-start(bf16[256,1024]{1,0:T(8,128)(2,1)} %collective-permute-done.11), channel_id=1, source_target_pairs={{8,24},{10,26},{12,28},{14,30},{24,8},{26,10},{28,12},{30,14},{9,2... | collective-permute-start | bytes 1572872 | tf_op jit(solution)/shard_map/ppermute | solution.py:67
  217.9 9.3 %collective-permute-done.21 = bf16[256,1024]{1,0:T(8,128)(2,1)S(1)} collective-permute-done((bf16[256,1024]{1,0:T(8,128)(2,1)}, bf16[256,1024]{1,0:T(8,128)(2,1)S(1)}, u32[]{:S(2)}, u32[]{:S(2)}) %collective-permute-start.21) | collective-permute-done | bytes 524320 | tf_op jit(solution)/shard_map/ppermute | solution.py:67
  227.8 3.4 %collective-permute-start.25 = (bf16[256,1024]{1,0:T(8,128)(2,1)S(1)}, bf16[256,1024]{1,0:T(8,128)(2,1)S(1)}, u32[]{:S(2)}, u32[]{:S(2)}) collective-permute-start(bf16[256,1024]{1,0:T(8,128)(2,1)S(1)} %collective-permute-done.13), channel_id=1, source_target_pairs={{12,28},{14,30},{28,12},{30,14},{13,29},{15,31},{29,13},{31,15}} | collective-permute-start | bytes 1572872 | tf_op jit(solution)/shard_map/ppermute | solution.py:67
  231.4 6.9 %collective-permute-done.23 = bf16[256,1024]{1,0:T(8,128)(2,1)S(1)} collective-permute-done((bf16[256,1024]{1,0:T(8,128)(2,1)}, bf16[256,1024]{1,0:T(8,128)(2,1)S(1)}, u32[]{:S(2)}, u32[]{:S(2)}) %collective-permute-start.23) | collective-permute-done | bytes 524320 | tf_op jit(solution)/shard_map/ppermute | solution.py:67
  238.4 3.6 %collective-permute-start.27 = (bf16[256,1024]{1,0:T(8,128)(2,1)S(1)}, bf16[256,1024]{1,0:T(8,128)(2,1)S(1)}, u32[]{:S(2)}, u32[]{:S(2)}) collective-permute-start(bf16[256,1024]{1,0:T(8,128)(2,1)S(1)} %collective-permute-done.14), channel_id=1, source_target_pairs={{12,28},{14,30},{28,12},{30,14},{13,29},{15,31},{29,13},{31,15}} | collective-permute-start | bytes 1572872 | tf_op jit(solution)/shard_map/ppermute | solution.py:67
  242.5 7.1 %collective-permute-done.25 = bf16[256,1024]{1,0:T(8,128)(2,1)S(1)} collective-permute-done((bf16[256,1024]{1,0:T(8,128)(2,1)S(1)}, bf16[256,1024]{1,0:T(8,128)(2,1)S(1)}, u32[]{:S(2)}, u32[]{:S(2)}) %collective-permute-start.25) | collective-permute-done | bytes 524320 | tf_op jit(solution)/shard_map/ppermute | solution.py:67
  249.8 8.4 %collective-permute-done.27 = bf16[256,1024]{1,0:T(8,128)(2,1)S(1)} collective-permute-done((bf16[256,1024]{1,0:T(8,128)(2,1)S(1)}, bf16[256,1024]{1,0:T(8,128)(2,1)S(1)}, u32[]{:S(2)}, u32[]{:S(2)}) %collective-permute-start.27) | collective-permute-done | bytes 524320 | tf_op jit(solution)/shard_map/ppermute | solution.py:67
  258.4 3.4 %fusion.10 = f32[768,1024]{1,0:T(8,128)S(1)} fusion(bf16[2048,1024]{1,0:T(8,128)(2,1)S(1)} %select_dynamic-update-slice_fusion, bf16[768,512]{1,0:T(8,128)(2,1)S(1)} %get-tuple-element.20, bf16[768,512]{1,0:T(8,128)(2,1)S(1)} %get-tuple-element.21, bf16[768,512]{1,0:T(8,128)(2,1)S(1)} %get-tuple-element.22, bf16[768,512]{1,0:T(8,128)(2,1)S(1)} %get-tuple-element.19), kind=kOutput, calls=%fused_computation.29 | convolution fusion | flops 3233808384 | bytes 10485760 | tf_op jit(solution)/shard_map/dot_general | solution.py:168
  264.8 4.4 %fusion.2 = bf16[1,4096,1024]{2,1,0:T(8,128)(2,1)} fusion(bf16[1,4096,1024]{2,1,0:T(8,128)(2,1)S(1)} %bitcast.55, f32[1024]{0:T(1024)S(1)} %slice.104, f32[4096]{0:T(1024)S(1)} %bitcast.66), kind=kLoop, calls=%fused_computation.4 | loop fusion | flops 16777216 | bytes 16797696 | tf_op jit(solution)/shard_map/convert_element_type | solution.py:141
  276.4 15.2 %collective-permute-done.16 = f32[384,512]{1,0:T(8,128)S(1)} collective-permute-done((f32[384,512]{1,0:T(8,128)S(1)}, f32[384,512]{1,0:T(8,128)S(1)}, u32[]{:S(2)}, u32[]{:S(2)}) %collective-permute-start.16) | collective-permute-done | bytes 786464 | tf_op jit(solution)/shard_map/ppermute | solution.py:173
  291.6 16.4 %collective-permute-done.30 = f32[384,512]{1,0:T(8,128)S(1)} collective-permute-done((f32[384,512]{1,0:T(8,128)S(1)}, f32[384,512]{1,0:T(8,128)S(1)}, u32[]{:S(2)}, u32[]{:S(2)}) %collective-permute-start.30) | collective-permute-done | bytes 786464 | tf_op jit(solution)/shard_map/ppermute | solution.py:173
  (146 shorter events, 78.9 us)
Async XLA Ops:
  7.2 155.4 %all-reduce.4.cloned.1.call-start = ((), (), s32[]{:S(2)}) async-start(), calls=%async_computation | async-start | bytes 2621440 | tf_op jit(solution)/shard_map/psum | solution.py:116
  11.8 77.8 %collective-permute-start.4 = (bf16[256,1024]{1,0:T(8,128)(2,1)}, bf16[256,1024]{1,0:T(8,128)(2,1)}, u32[]{:S(2)}, u32[]{:S(2)}) collective-permute-start(bf16[256,1024]{1,0:T(8,128)(2,1)} %get-tuple-element.27), channel_id=1, source_target_pairs={{4,0},{6,2},{8,4},{10,6},{12,8},{14,10},{20,16},{22,18},{24,20},{2... | collective-permute-start | bytes 1572872 | tf_op jit(solution)/shard_map/ppermute | solution.py:58
  15.0 94.2 %collective-permute-start.3 = (bf16[256,1024]{1,0:T(8,128)(2,1)}, bf16[256,1024]{1,0:T(8,128)(2,1)}, u32[]{:S(2)}, u32[]{:S(2)}) collective-permute-start(bf16[256,1024]{1,0:T(8,128)(2,1)} %get-tuple-element.27), channel_id=1, source_target_pairs={{0,4},{2,6},{4,8},{6,10},{8,12},{10,14},{16,20},{18,22},{20,24},{2... | collective-permute-start | bytes 1572872 | tf_op jit(solution)/shard_map/ppermute | solution.py:58
  16.3 78.3 %collective-permute-start.8 = (bf16[256,1024]{1,0:T(8,128)(2,1)}, bf16[256,1024]{1,0:T(8,128)(2,1)}, u32[]{:S(2)}, u32[]{:S(2)}) collective-permute-start(bf16[256,1024]{1,0:T(8,128)(2,1)} %get-tuple-element.26), channel_id=1, source_target_pairs={{4,0},{6,2},{8,4},{10,6},{12,8},{14,10},{20,16},{22,18},{24,20},{2... | collective-permute-start | bytes 1572872 | tf_op jit(solution)/shard_map/ppermute | solution.py:58
  21.7 88.8 %collective-permute-start.7 = (bf16[256,1024]{1,0:T(8,128)(2,1)}, bf16[256,1024]{1,0:T(8,128)(2,1)}, u32[]{:S(2)}, u32[]{:S(2)}) collective-permute-start(bf16[256,1024]{1,0:T(8,128)(2,1)} %get-tuple-element.26), channel_id=1, source_target_pairs={{0,4},{2,6},{4,8},{6,10},{8,12},{10,14},{16,20},{18,22},{20,24},{2... | collective-permute-start | bytes 1572872 | tf_op jit(solution)/shard_map/ppermute | solution.py:58
  94.7 17.2 %collective-permute-start.9 = (bf16[256,1024]{1,0:T(8,128)(2,1)}, bf16[256,1024]{1,0:T(8,128)(2,1)}, u32[]{:S(2)}, u32[]{:S(2)}) collective-permute-start(bf16[256,1024]{1,0:T(8,128)(2,1)} %collective-permute-done.8), channel_id=1, source_target_pairs={{4,0},{6,2},{8,4},{10,6},{20,16},{22,18},{24,20},{26,22},{5,1},{7,... | collective-permute-start | bytes 1572872 | tf_op jit(solution)/shard_map/ppermute | solution.py:58
  101.0 63.1 %collective-permute-start.6 = (bf16[256,1024]{1,0:T(8,128)(2,1)}, bf16[256,1024]{1,0:T(8,128)(2,1)}, u32[]{:S(2)}, u32[]{:S(2)}) collective-permute-start(bf16[256,1024]{1,0:T(8,128)(2,1)} %collective-permute-done.5), channel_id=1, source_target_pairs={{4,0},{6,2},{20,16},{22,18},{5,1},{7,3},{21,17},{23,19}} | collective-permute-start | bytes 1572872 | tf_op jit(solution)/shard_map/ppermute | solution.py:58
  108.0 92.2 %collective-permute-start.1 = (bf16[384,2048]{1,0:T(8,128)(2,1)}, bf16[384,2048]{1,0:T(8,128)(2,1)S(1)}, u32[]{:S(2)}, u32[]{:S(2)}) collective-permute-start(bf16[384,2048]{1,0:T(8,128)(2,1)} %bitcast.60), channel_id=1, source_target_pairs={{0,2},{2,0},{4,6},{6,4},{8,10},{10,8},{12,14},{14,12},{1,3},{3,1},... | collective-permute-start | bytes 4718600 | tf_op jit(solution)/shard_map/ppermute | solution.py:109
  109.2 60.4 %collective-permute-start.11 = (bf16[256,1024]{1,0:T(8,128)(2,1)}, bf16[256,1024]{1,0:T(8,128)(2,1)}, u32[]{:S(2)}, u32[]{:S(2)}) collective-permute-start(bf16[256,1024]{1,0:T(8,128)(2,1)} %collective-permute-done.3), channel_id=1, source_target_pairs={{4,8},{6,10},{8,12},{10,14},{20,24},{22,26},{24,28},{26,30},{5,9},... | collective-permute-start | bytes 1572872 | tf_op jit(solution)/shard_map/ppermute | solution.py:58
  110.5 61.5 %collective-permute-start.12 = (bf16[256,1024]{1,0:T(8,128)(2,1)}, bf16[256,1024]{1,0:T(8,128)(2,1)}, u32[]{:S(2)}, u32[]{:S(2)}) collective-permute-start(bf16[256,1024]{1,0:T(8,128)(2,1)} %collective-permute-done.7), channel_id=1, source_target_pairs={{4,8},{6,10},{8,12},{10,14},{20,24},{22,26},{24,28},{26,30},{5,9},... | collective-permute-start | bytes 1572872 | tf_op jit(solution)/shard_map/ppermute | solution.py:58
  111.8 61.5 %collective-permute-start.10 = (bf16[256,1024]{1,0:T(8,128)(2,1)}, bf16[256,1024]{1,0:T(8,128)(2,1)}, u32[]{:S(2)}, u32[]{:S(2)}) collective-permute-start(bf16[256,1024]{1,0:T(8,128)(2,1)} %collective-permute-done.9), channel_id=1, source_target_pairs={{4,0},{6,2},{20,16},{22,18},{5,1},{7,3},{21,17},{23,19}} | collective-permute-start | bytes 1572872 | tf_op jit(solution)/shard_map/ppermute | solution.py:58
  164.1 46.0 %collective-permute-start.17 = (bf16[256,1024]{1,0:T(8,128)(2,1)}, bf16[256,1024]{1,0:T(8,128)(2,1)S(1)}, u32[]{:S(2)}, u32[]{:S(2)}) collective-permute-start(bf16[256,1024]{1,0:T(8,128)(2,1)} %collective-permute-done.3), channel_id=1, source_target_pairs={{4,20},{6,22},{8,24},{10,26},{12,28},{14,30},{20,4},{22,6},{24,8},... | collective-permute-start | bytes 1572872 | tf_op jit(solution)/shard_map/ppermute | solution.py:67
  169.6 44.9 %collective-permute-start.19 = (bf16[256,1024]{1,0:T(8,128)(2,1)}, bf16[256,1024]{1,0:T(8,128)(2,1)S(1)}, u32[]{:S(2)}, u32[]{:S(2)}) collective-permute-start(bf16[256,1024]{1,0:T(8,128)(2,1)} %collective-permute-done.7), channel_id=1, source_target_pairs={{4,20},{6,22},{8,24},{10,26},{12,28},{14,30},{20,4},{22,6},{24,8},... | collective-permute-start | bytes 1572872 | tf_op jit(solution)/shard_map/ppermute | solution.py:67
  173.4 25.2 %collective-permute-start.14 = (bf16[256,1024]{1,0:T(8,128)(2,1)}, bf16[256,1024]{1,0:T(8,128)(2,1)S(1)}, u32[]{:S(2)}, u32[]{:S(2)}) collective-permute-start(bf16[256,1024]{1,0:T(8,128)(2,1)} %collective-permute-done.12), channel_id=1, source_target_pairs={{8,12},{10,14},{24,28},{26,30},{9,13},{11,15},{25,29},{27,31}} | collective-permute-start | bytes 1572872 | tf_op jit(solution)/shard_map/ppermute | solution.py:58
  189.0 53.2 %collective-permute-start.26 = (bf16[256,1024]{1,0:T(8,128)(2,1)}, bf16[256,1024]{1,0:T(8,128)(2,1)S(1)}, u32[]{:S(2)}, u32[]{:S(2)}) collective-permute-start(bf16[256,1024]{1,0:T(8,128)(2,1)} %collective-permute-done.4), channel_id=1, source_target_pairs={{0,16},{2,18},{4,20},{6,22},{8,24},{10,26},{16,0},{18,2},{20,4},{2... | collective-permute-start | bytes 1572872 | tf_op jit(solution)/shard_map/ppermute | solution.py:67
  214.5 23.9 %collective-permute-start.23 = (bf16[256,1024]{1,0:T(8,128)(2,1)}, bf16[256,1024]{1,0:T(8,128)(2,1)S(1)}, u32[]{:S(2)}, u32[]{:S(2)}) collective-permute-start(bf16[256,1024]{1,0:T(8,128)(2,1)} %collective-permute-done.12), channel_id=1, source_target_pairs={{8,24},{10,26},{12,28},{14,30},{24,8},{26,10},{28,12},{30,14},{9,2... | collective-permute-start | bytes 1572872 | tf_op jit(solution)/shard_map/ppermute | solution.py:67
  217.0 21.4 %collective-permute-start.24 = (bf16[256,1024]{1,0:T(8,128)(2,1)}, bf16[256,1024]{1,0:T(8,128)(2,1)S(1)}, u32[]{:S(2)}, u32[]{:S(2)}) collective-permute-start(bf16[256,1024]{1,0:T(8,128)(2,1)} %collective-permute-done.9), channel_id=1, source_target_pairs={{0,16},{2,18},{4,20},{6,22},{16,0},{18,2},{20,4},{22,6},{1,17},{3,... | collective-permute-start | bytes 1572872 | tf_op jit(solution)/shard_map/ppermute | solution.py:67
  227.1 22.7 %collective-permute-start.28 = (bf16[256,1024]{1,0:T(8,128)(2,1)}, bf16[256,1024]{1,0:T(8,128)(2,1)S(1)}, u32[]{:S(2)}, u32[]{:S(2)}) collective-permute-start(bf16[256,1024]{1,0:T(8,128)(2,1)} %collective-permute-done.8), channel_id=1, source_target_pairs={{0,16},{2,18},{4,20},{6,22},{8,24},{10,26},{16,0},{18,2},{20,4},{2... | collective-permute-start | bytes 1572872 | tf_op jit(solution)/shard_map/ppermute | solution.py:67
  227.8 21.8 %collective-permute-start.25 = (bf16[256,1024]{1,0:T(8,128)(2,1)S(1)}, bf16[256,1024]{1,0:T(8,128)(2,1)S(1)}, u32[]{:S(2)}, u32[]{:S(2)}) collective-permute-start(bf16[256,1024]{1,0:T(8,128)(2,1)S(1)} %collective-permute-done.13), channel_id=1, source_target_pairs={{12,28},{14,30},{28,12},{30,14},{13,29},{15,31},{29,13},{31,15}} | collective-permute-start | bytes 1572872 | tf_op jit(solution)/shard_map/ppermute | solution.py:67
  238.4 30.8 %collective-permute-start = (f32[80]{0:T(128)S(1)}, f32[80]{0:T(128)S(1)}, u32[]{:S(2)}, u32[]{:S(2)}) collective-permute-start(f32[80]{0:T(128)S(1)} %multiply_reduce_fusion), channel_id=1, source_target_pairs={{0,1},{1,0},{2,3},{3,2},{4,5},{5,4},{6,7},{7,6},{8,9},{9,8},{10,11... | collective-permute-start | bytes 968 | tf_op jit(solution)/shard_map/ppermute | solution.py:118
  238.4 19.8 %collective-permute-start.27 = (bf16[256,1024]{1,0:T(8,128)(2,1)S(1)}, bf16[256,1024]{1,0:T(8,128)(2,1)S(1)}, u32[]{:S(2)}, u32[]{:S(2)}) collective-permute-start(bf16[256,1024]{1,0:T(8,128)(2,1)S(1)} %collective-permute-done.14), channel_id=1, source_target_pairs={{12,28},{14,30},{28,12},{30,14},{13,29},{15,31},{29,13},{31,15}} | collective-permute-start | bytes 1572872 | tf_op jit(solution)/shard_map/ppermute | solution.py:67
  242.2 27.0 %collective-permute-start.15 = (f32[768,512]{1,0:T(8,128)}, f32[768,512]{1,0:T(8,128)}, u32[]{:S(2)}, u32[]{:S(2)}) collective-permute-start(f32[768,512]{1,0:T(8,128)} %constant_dynamic-slice_fusion.1), channel_id=1, source_target_pairs={{0,1},{1,0},{2,3},{3,2},{4,5},{5,4},{6,7},{7,6},{8,9},{9,8},{10,11... | collective-permute-start | bytes 4718600 | tf_op jit(solution)/shard_map/ppermute | solution.py:172
  271.2 20.4 %collective-permute-start.16 = (f32[384,512]{1,0:T(8,128)S(1)}, f32[384,512]{1,0:T(8,128)S(1)}, u32[]{:S(2)}, u32[]{:S(2)}) collective-permute-start(f32[384,512]{1,0:T(8,128)S(1)} %slice.101), channel_id=1, source_target_pairs={{0,2},{2,0},{4,6},{6,4},{8,10},{10,8},{12,14},{14,12},{1,3},{3,1},... | collective-permute-start | bytes 2359304 | tf_op jit(solution)/shard_map/ppermute | solution.py:173
  274.3 33.7 %collective-permute-start.30 = (f32[384,512]{1,0:T(8,128)S(1)}, f32[384,512]{1,0:T(8,128)S(1)}, u32[]{:S(2)}, u32[]{:S(2)}) collective-permute-start(f32[384,512]{1,0:T(8,128)S(1)} %slice.103), channel_id=1, source_target_pairs={{0,2},{2,0},{4,6},{6,4},{8,10},{10,8},{12,14},{14,12},{1,3},{3,1},... | collective-permute-start | bytes 2359304 | tf_op jit(solution)/shard_map/ppermute | solution.py:173
  (20 other events, 203.9 us)
Sparse Core Ops, SparseCore 0:
  74.2 88.3 all-reduce.3

commit v3 on v2

--- a/solution.py
+++ b/solution.py
@@ -1,13 +1,17 @@
+import functools
 import math
 
 import jax
 import jax.numpy as jnp
 from jax import lax
+from jax.experimental import pallas as pl
+from jax.experimental.pallas import tpu as pltpu
 from jax.sharding import PartitionSpec as P
 
+MESH = pl.DeviceIdType.MESH
+
 
 def direction_parts(residual, lengths, labels, earlier_means, chosen):
-    highest = lax.Precision.HIGHEST
     length = residual.shape[1]
     positions = jnp.arange(length, dtype=jnp.int32)
     valid_mask = (positions[None, :] < lengths[:, None]).astype(jnp.bfloat16)
@@ -22,7 +26,16 @@
         earlier, jnp.minimum(chosen[0], layers - 2), 0, keepdims=False
     )
     picked = jnp.where(chosen[0] == layers - 1, current, picked)
-    weighted, totals = lax.psum((counts[:, None] * picked, counts), "dp")
+    packed = jnp.concatenate(
+        [
+            (counts[:, None] * picked).reshape(-1, 128),
+            jnp.broadcast_to(jnp.repeat(counts, 4)[:, None], (8, 128)),
+        ],
+        axis=0,
+    )
+    gathered = jnp.sum(gather_small(packed), axis=0)
+    totals = gathered[-8::4, 0]
+    weighted = gathered[:-8].reshape(2, -1)
     merged = weighted / totals[:, None]
     picked_difference = merged[1] - merged[0]
     share = counts / totals
@@ -40,53 +53,191 @@
     return [(i, i ^ 1) for i in range(axis_size)]
 
 
-def chain_pieces(own, groups, width, parts):
-    lines = width // 2
-    axes = ("groups", "dp")
-    rows = own.shape[0] // parts
-    place = lax.axis_index("dp") // 2
-
-    def hop(value, step, way):
-        pairs = []
-        for g in range(groups):
-            for j in range(width):
-                z = j // 2
-                if way > 0 and step - 1 <= z < lines - 1:
-                    pairs.append((g * width + j, g * width + j + 2))
-                if way < 0 and 0 < z <= lines - step:
-                    pairs.append((g * width + j, g * width + j - 2))
-        return lax.ppermute(value, axes, pairs)
-
-    def cross(value, step, way):
-        pairs = []
-        for g in range(groups):
-            for j in range(width):
-                z = j // 2
-                if (way > 0 and z >= step) or (way < 0 and z < lines - step):
-                    pairs.append((g * width + j, (g ^ 1) * width + j))
-        return lax.ppermute(value, axes, pairs)
-
-    chain = {}
-    crossed = {}
-    for way in (1, -1):
-        for part in range(parts):
-            chain[way, 0, part] = own[part * rows : (part + 1) * rows]
+def gather_kernel(peers, mine_ref, all_ref, own_sem, send_sem, recv_sem):
+    me = lax.axis_index("dp")
+    barrier = pltpu.get_barrier_semaphore()
+    for far in range(1, peers):
+        pl.semaphore_signal(
+            barrier, inc=1, device_id={"dp": lax.rem(me + far, peers)}, device_id_type=MESH
+        )
+    pl.semaphore_wait(barrier, peers - 1)
+    own = pltpu.make_async_copy(mine_ref, all_ref.at[me], own_sem)
+    own.start()
+    copies = []
+    for far in range(1, peers):
+        copies.append(
+            pltpu.make_async_remote_copy(
+                src_ref=mine_ref,
+                dst_ref=all_ref.at[me],
+                send_sem=send_sem.at[far],
+                recv_sem=recv_sem.at[far],
+                device_id={"dp": lax.rem(me + far, peers)},
+                device_id_type=MESH,
+            )
+        )
+        copies[-1].start()
+    own.wait()
+    for copy in copies:
+        copy.wait_send()
+        copy.wait_recv()
+
+
+def gather_small(value):
+    peers = lax.axis_size("dp")
+    return pl.pallas_call(
+        functools.partial(gather_kernel, peers),
+        out_shape=jax.ShapeDtypeStruct((peers,) + value.shape, value.dtype),
+        in_specs=[pl.BlockSpec(memory_space=pltpu.VMEM)],
+        out_specs=pl.BlockSpec(memory_space=pltpu.VMEM),
+        scratch_shapes=[
+            pltpu.SemaphoreType.DMA,
+            pltpu.SemaphoreType.DMA((peers,)),
+            pltpu.SemaphoreType.DMA((peers,)),
+        ],
+        compiler_params=pltpu.CompilerParams(collective_id=0, has_side_effects=True),
+        name="gather_small",
+    )(value)
+
+
+def chain_kernel(
+    lines, parts, chain_own, cross_own, wanted, chain_ref, cross_ref, rows_ref, own_sem,
+    swap_sem, hop_send, hop_recv, cross_send, cross_recv,
+):
+    width = 2 * lines
+    group, me = lax.axis_index("groups"), lax.axis_index("dp")
+    place = me // 2
+    beside = me + 1 - 2 * lax.rem(me, 2)
+    across = group + 1 - 2 * lax.rem(group, 2)
+    rows = chain_own.shape[0] // parts
+    barrier = pltpu.get_barrier_semaphore()
+
+    for far in range(1, width):
+        pl.semaphore_signal(
+            barrier, inc=1, device_id={"dp": lax.rem(me + far, width)}, device_id_type=MESH
+        )
+    pl.semaphore_signal(barrier, inc=1, device_id={"groups": across}, device_id_type=MESH)
+    pl.semaphore_wait(barrier, width)
+
+    def hop(step, part, way):
+        k = 0 if way > 0 else 1
+        slot = lax.rem(place - way * (step - 1) + lines, lines)
+        here = pl.ds(part * rows, rows)
+        source = chain_own.at[here] if step == 1 else chain_ref.at[slot, here]
+        return pltpu.make_async_remote_copy(
+            src_ref=source,
+            dst_ref=chain_ref.at[slot, here],
+            send_sem=hop_send.at[k, step, part],
+            recv_sem=hop_recv.at[k, step, part],
+            device_id={"dp": lax.rem(me + 2 * way + width, width)},
+            device_id_type=MESH,
+        )
+
+    def arrival(step, part, way):
+        k = 0 if way > 0 else 1
+        slot = lax.rem(place - way * step + lines, lines)
+        here = pl.ds(part * rows, rows)
+        landed = chain_ref.at[slot, here]
+        return pltpu.make_async_remote_copy(
+            src_ref=landed,
+            dst_ref=landed,
+            send_sem=hop_send.at[k, step, part],
+            recv_sem=hop_recv.at[k, step, part],
+            device_id={"dp": lax.rem(me - 2 * way + width, width)},
+            device_id_type=MESH,
+        )
+
+    def cross(step, part, way):
+        k = 0 if way > 0 else 1
+        slot = lax.rem(place - way * step + lines, lines)
+        here = pl.ds(part * rows, rows)
+        return pltpu.make_async_remote_copy(
+            src_ref=chain_ref.at[slot, here],
+            dst_ref=cross_ref.at[slot, here],
+            send_sem=cross_send.at[k, step, part],
+            recv_sem=cross_recv.at[k, step, part],
+            device_id={"groups": across},
+            device_id_type=MESH,
+        )
+
+    def sends(step, way):
+        return (place >= step - 1) & (place < lines - 1) if way > 0 else (
+            (place > 0) & (place <= lines - step)
+        )
+
+    def holds(step, way):
+        return place >= step if way > 0 else place < lines - step
+
+    for part in range(parts):
+        for way in (1, -1):
+
+            @pl.when(sends(1, way))
+            def _():
+                hop(1, part, way).start()
+
+    swap = pltpu.make_async_remote_copy(
+        src_ref=wanted,
+        dst_ref=rows_ref,
+        send_sem=swap_sem.at[0],
+        recv_sem=swap_sem.at[1],
+        device_id={"dp": beside},
+        device_id_type=MESH,
+    )
+    swap.start()
+    keep_chain = pltpu.make_async_copy(chain_own, chain_ref.at[place], own_sem.at[0])
+    keep_cross = pltpu.make_async_copy(cross_own, cross_ref.at[place], own_sem.at[1])
+    keep_chain.start()
+    keep_cross.start()
+
     for step in range(1, lines):
         for part in range(parts):
             for way in (1, -1):
-                chain[way, step, part] = hop(chain[way, step - 1, part], step, way)
-                crossed[way, step, part] = cross(chain[way, step, part], step, way)
-
-    def merged(table):
-        blocks = []
-        for step in range(1, lines):
-            for part in range(parts):
-                blocks.append(
-                    jnp.where(place >= step, table[1, step, part], table[-1, lines - step, part])
-                )
-        return blocks
-
-    return merged(chain), merged(crossed)
+
+                @pl.when(holds(step, way))
+                def _():
+                    arrival(step, part, way).wait_recv()
+                    if step < lines - 1:
+
+                        @pl.when(sends(step + 1, way))
+                        def _():
+                            hop(step + 1, part, way).start()
+
+                    cross(step, part, way).start()
+
+    keep_chain.wait()
+    keep_cross.wait()
+    swap.wait_send()
+    swap.wait_recv()
+    for step in range(1, lines):
+        for part in range(parts):
+            for way in (1, -1):
+
+                @pl.when(sends(step, way))
+                def _():
+                    hop(step, part, way).wait_send()
+
+                @pl.when(holds(step, way))
+                def _():
+                    cross(step, part, way).wait_send()
+                    cross(step, part, way).wait_recv()
+
+
+def chain_gather(chain_own, cross_own, wanted, lines, parts):
+    full = jax.ShapeDtypeStruct((lines,) + chain_own.shape, chain_own.dtype)
+    any_spec = pl.BlockSpec(memory_space=pl.ANY)
+    return pl.pallas_call(
+        functools.partial(chain_kernel, lines, parts),
+        out_shape=(full, full, jax.ShapeDtypeStruct(wanted.shape, wanted.dtype)),
+        in_specs=[any_spec] * 3,
+        out_specs=[any_spec] * 3,
+        scratch_shapes=[
+            pltpu.SemaphoreType.DMA((2,)),
+            pltpu.SemaphoreType.DMA((2,)),
+        ]
+        + [pltpu.SemaphoreType.DMA((2, lines, parts))] * 4,
+        compiler_params=pltpu.CompilerParams(collective_id=1, has_side_effects=True),
+        cost_estimate=pl.CostEstimate(flops=0, transcendentals=0, bytes_accessed=200 << 20),
+        name="chain_gather",
+    )(chain_own, cross_own, wanted)
 
 
 def shards(
@@ -99,24 +250,19 @@
     lines = width // 2
     block = half_width // width
     even = lax.axis_index("groups") % 2 == 0
-    place = lax.axis_index("dp") // 2
     side = lax.axis_index("dp") % 2
     core = lax.axis_index("mp")
 
     token_rows = residual.reshape(tokens, half_width)
     blocked = token_rows.reshape(tokens, lines, 2 * block)
     wanted = lax.dynamic_slice_in_dim(blocked, (1 - side) * block, block, 2)
-    neighbour_rows = lax.ppermute(wanted.reshape(tokens, lines * block), "dp", pair_perm(width))
     key_own, value_own = key_weight[0], value_weight[0]
     chain_own = jnp.where(even, key_own, value_own)
     cross_own = jnp.where(even, value_own, key_own)
-    chain, crossed = chain_pieces(chain_own, groups, width, 2)
-
     picked_difference, local = direction_parts(residual, lengths, labels, earlier_means, chosen)
+    local, wanted = lax.optimization_barrier((local, wanted.reshape(tokens, lines * block)))
     difference = lax.psum(local, "dp")
-    square_half = jnp.sum(difference * difference, axis=1)
-    square_sums = square_half + lax.ppermute(square_half, "mp", pair_perm(2))
-    directions = difference * lax.rsqrt(square_sums / model_width + 1e-06)[:, None]
+    chain, crossed, neighbour_rows = chain_gather(chain_own, cross_own, wanted, lines, 4)
 
     local_square = jnp.sum(picked_difference * picked_difference)
     local_mean = local_square / half_width + 1e-06
@@ -155,17 +301,9 @@
         * both[1][:, None]
         * feature_part(norm_gain).reshape(1, -1)
     ).astype(jnp.bfloat16)
-    ordered = jnp.concatenate(
-        [
-            lax.dynamic_slice_in_dim(normed, (place - step + lines) % lines * block, block, 1)
-            for step in range(lines)
-        ],
-        axis=1,
-    )
-
-    def finish(own, blocks):
-        weight = jnp.concatenate([own] + blocks, axis=0)
-        total = jnp.dot(ordered, weight, preferred_element_type=jnp.float32)
+    def finish(weight):
+        weight = weight.reshape(lines * block, -1)
+        total = jnp.dot(normed, weight, preferred_element_type=jnp.float32)
         half = total.shape[1] // 2
         away = lax.dynamic_slice_in_dim(total, (1 - core) * half, half, 1)
         kept = lax.dynamic_slice_in_dim(total, core * half, half, 1)
@@ -173,8 +311,13 @@
         result = kept[:tokens] + lax.ppermute(kept[tokens:], "dp", pair_perm(width))
         return result.astype(jnp.bfloat16).reshape(prompts, length, half)
 
-    chain_out = finish(chain_own, chain)
-    cross_out = finish(cross_own, crossed)
+    chain_out = finish(chain)
+    cross_out = finish(crossed)
+    difference, normed = lax.optimization_barrier((difference, normed))
+    square_half = jnp.sum(difference * difference, axis=1)
+    square_sums = square_half + lax.ppermute(square_half, "mp", pair_perm(2))
+    directions = difference * lax.rsqrt(square_sums / model_width + 1e-06)[:, None]
+
     key_cache = jnp.where(even, chain_out, cross_out)
     value_cache = jnp.where(even, cross_out, chain_out)
     return (directions, key_cache, value_cache, ortho_proj)

time: 318 us -> 251 us (0.79); the launches traced: 317 us -> 246 us
  Pallas kernels: 0 us -> 112 us
  waiting for transfers between devices: 129 us -> 31.7 us
  starting transfers between devices: 49.8 us -> 4.69 us
  blocking collectives: 43.3 us -> 6.07 us
    pallas_call x0 -> x2, Pallas kernels: none -> 112 us  [the longest x1 100 us: chain_gather(): pl.pallas_call(functools.partial(chain_kernel, lines, parts), out_shape=(...]
    psum x1, waiting for transfers between devices: 49.3 us -> 0.01 us  [shards(): difference = lax.psum(local, 'dp')]
    ppermute x25 -> x0, waiting for transfers between devices: 47.8 us -> none  [the longest x12 31.7 us: cross(): return lax.ppermute(value, axes, pairs)]
    ppermute x25 -> x0, starting transfers between devices: 46.4 us -> none  [the longest x12 22.8 us: cross(): return lax.ppermute(value, axes, pairs)]
    psum x1 -> x0, blocking collectives: 37.5 us -> none  [direction_parts(): weighted, totals = lax.psum((counts[:, None] * picked, counts), 'dp')]
    unnamed x13 -> x1, other arithmetic: 14.4 us -> 0.77 us
    unnamed x32 -> x26, local copies, waits for them, and re-layouts: 10.9 us -> 7.4 us
    convert_element_type x1, other arithmetic: 4.44 us -> 7.83 us  [shards(): (matrix.astype(jnp.float32) - refusal_dir[:, None] * column_proj[None, :]...]
  transfers between devices with their start and end apart: 32 -> 7, of which waited for: 9 -> 2; matrix products, arithmetic and copies ran while one was open for 21% -> 17% of each run, Pallas kernels for 0% -> 41%
where the time goes in v3:
time: 251 us; the launch traced here: 246 us
  Pallas kernels  112 us (45%)
  other arithmetic  44 us (18%)
  waiting for transfers between devices  31.7 us (13%)
  local copies, waits for them, and re-layouts  23.3 us (9%)
  between operations  17.1 us (7%)
  matrix products  7.36 us (3%)
  blocking collectives  6.07 us (2%)
  starting transfers between devices  4.69 us (2%)
    pallas_call x1, Pallas kernels, chain_gather(): pl.pallas_call(functools.partial(chain_kernel, lines, parts), out_shape=(...  100 us
    ppermute x2, waiting for transfers between devices, finish(): result = kept[:tokens] + lax.ppermute(kept[tokens:], 'dp', pair_perm(width))  31.6 us
    pallas_call x1, Pallas kernels, gather_small(): pl.pallas_call(functools.partial(gather_kernel, peers), out_shape=jax.Sha...  11.9 us
    convert_element_type x1, other arithmetic, shards(): (matrix.astype(jnp.float32) - refusal_dir[:, None] * column_proj[None, :]...  7.83 us
    unnamed x26, local copies, waits for them, and re-layouts  7.4 us
    dot_general x2, matrix products, finish(): total = jnp.dot(normed, weight, preferred_element_type=jnp.float32)  6.84 us
    another operation x1, local copies, waits for them, and re-layouts, shards(): blocked = token_rows.reshape(tokens, lines, 2 * block)  6.3 us
    reduce_sum x1, other arithmetic, shards(): columns = jnp.sum(matrix.astype(jnp.float32) * unit[:, None], axis=0)  5.09 us
  transfers between devices with their start and end apart: 7, of which 2 were waited for; matrix products, arithmetic and copies ran while one was open for 17% of the time, Pallas kernels for 41%

profile of v3, /device:TPU:24, one launch (start us, length us, event | category | flops | bytes accessed | tf_op | source)
XLA Modules:
  0.0 246.3 jit_solution(1880458330640349911)
XLA Ops:
  10.1 6.3 %reshape_reshape.3 = bf16[384,4,1024]{2,1,0:T(4,128)(2,1)} reshape(bf16[3,128,4096]{2,1,0:T(8,128)(2,1)} %param.9) | data formatting | bytes 6291456 | tf_op jit(solution)/shard_map/reshape;reshape | solution.py:257
  18.0 4.7 %copy.28 = f32[1,79,2,4096]{3,1,2,0:T(8,128)} copy(f32[1,79,2,4096]{3,2,1,0:T(2,128)} %param.12) | data formatting | bytes 5177344 | tf_op args[3]
  24.7 11.9 %gather_small.1 = f32[8,72,128]{2,1,0:T(8,128)} custom-call(f32[72,128]{1,0:T(8,128)} %pad_maximum_fusion.1.mine_ref), custom_call_target="tpu_custom_call" | custom-call | tf_op jit(solution)/shard_map/gather_small/pallas_call | solution.py:87
  39.6 4.2 %fusion.7 = f32[79,4096]{1,0:T(8,128)} fusion(f32[79,2,4096]{2,0,1:T(8,128)} %bitcast.50, f32[]{:T(128)} %bitcast.6, f32[]{:T(128)} %bitcast.4), kind=kLoop, calls=%fused_computation.16 | loop fusion | flops 970752 | bytes 3883016 | tf_op jit(solution)/shard_map/sub | solution.py:44
  43.8 4.1 %constant_dynamic-slice_fusion.2 = (bf16[384,4,512]{2,1,0:T(4,128)(2,1)}, bf16[384,4,512]{2,1,0:T(4,128)(2,1)S(1)}) fusion(bf16[384,4,1024]{2,1,0:T(4,128)(2,1)} %reshape_reshape.3, s32[]{:T(128)S(6)} %select_n.79, s32[]{:T(128)S(6)} %select_n.78), kind=kLoop, calls=%fused_computation.54 | loop fusion | bytes 6291464 | tf_op jit(solution)/shard_map/dynamic_slice | solution.py:293
  47.9 1.6 copy.20
  52.9 5.1 %fusion.1 = f32[1024]{0:T(1024)S(1)} fusion(bf16[1,4096,1024]{2,1,0:T(8,128)(2,1)} %param.17, f32[4096]{0:T(1024)S(1)} %bitcast.58), kind=kLoop, calls=%fused_computation.3 | loop fusion | flops 12581888 | bytes 8409088 | tf_op jit(solution)/shard_map/reduce_sum | solution.py:273
  60.0 3.3 %all-reduce = f32[2818]{0:T(1024)S(1)} all-reduce(f32[2818]{0:T(1024)S(1)} %maximum_dynamic-update-slice_fusion), channel_id=2, replica_groups=mesh['groups'=2,'dp'=8,'mp'=2] {'mp'}, use_global_device_ids=true, to_apply=%add | all-reduce | flops 2818 | bytes 22544
  67.3 2.8 %psum.15 = f32[384]{0:T(512)S(1)} all-reduce(f32[384]{0:T(512)S(1)} %bitcast.63), channel_id=1, replica_groups=mesh['groups'=2,'dp'=8,'mp'=2] {'mp'}, use_global_device_ids=true, to_apply=%region_10.11 | all-reduce | flops 384 | bytes 3072 | tf_op jit(solution)/shard_map/psum | solution.py:285
  70.1 1.9 collective-permute-start
  72.1 3.0 %select_bitcast_fusion = (bf16[512,1024]{1,0:T(8,128)(2,1)}, bf16[512,1024]{1,0:T(8,128)(2,1)}) fusion(bf16[1,512,1024]{2,1,0:T(8,128)(2,1)} %param.16, bf16[1,512,1024]{2,1,0:T(8,128)(2,1)} %param.15, pred[]{:T(512)S(6)} %eq.34), kind=kLoop, calls=%fused_computation.20 | loop fusion | flops 1048576 | bytes 4194305 | tf_op jit(solution)/shard_map/jit(_where)/select_n | solution.py:261
  75.6 100.4 %chain_gather.1 = (bf16[4,512,1024]{2,1,0:T(8,128)(2,1)}, bf16[4,512,1024]{2,1,0:T(8,128)(2,1)}, bf16[384,2048]{1,0:T(8,128)(2,1)}) custom-call(bf16[512,1024]{1,0:T(8,128)(2,1)} %get-tuple-element.28.chain_own, bf16[512,1024]{1,0:T(8,128)(2,1)} %get-tuple-element.27.cross_own, bf16[384,2048]{1,0:T(8,128)(2,1)} %bitcast.51), custom_call_target="tpu_custom_call" | custom-call | bytes 209715200 | tf_op jit(solution)/shard_map/chain_gather/pallas_call | solution.py:227
  176.0 2.7 %multiply_convert_fusion = bf16[768,2048]{1,0:T(8,128)(2,1)S(1)} fusion(bf16[384,2048]{1,0:T(8,128)(2,1)} %get-tuple-element.12, bf16[384,2048]{1,0:T(8,128)(2,1)S(1)} %bitcast.52, f32[2048]{0:T(1024)S(1)} %bitcast.61, f32[768]{0:T(1024)S(1)} %get-tuple-element.17, f32[2048]{0:T(1024)S(1)} %bitcast.62, f32[768]{0:T(1024)S(1)} %get-tuple-element.16), kind=kLoop, calls=%fused_computation.10 | loop fusion | flops 14155776 | bytes 6313984 | tf_op jit(solution)/shard_map/convert_element_type | solution.py:303
  178.8 3.4 %fusion.21 = f32[768,1024]{1,0:T(8,128)S(1)} fusion(bf16[768,2048]{1,0:T(8,128)(2,1)S(1)} %multiply_convert_fusion, bf16[2048,1024]{1,0:T(8,128)(2,1)S(1)} %bitcast.66), kind=kOutput, calls=%fused_computation.70 | convolution fusion | flops 3221225472 | bytes 10485760 | tf_op jit(solution)/shard_map/dot_general | solution.py:306
  182.2 1.4 constant_dynamic-slice_fusion
  183.7 3.4 %fusion.20 = f32[768,1024]{1,0:T(8,128)S(1)} fusion(bf16[768,2048]{1,0:T(8,128)(2,1)S(1)} %multiply_convert_fusion, bf16[2048,1024]{1,0:T(8,128)(2,1)S(1)} %bitcast.65), kind=kOutput, calls=%fused_computation.69 | convolution fusion | flops 3221225472 | bytes 10485760 | tf_op jit(solution)/shard_map/dot_general | solution.py:306
  187.1 1.3 constant_dynamic-slice_fusion.1
  188.9 1.5 multiply_reduce_fusion
  190.5 7.8 %fusion.2 = bf16[1,4096,1024]{2,1,0:T(8,128)(2,1)} fusion(bf16[1,4096,1024]{2,1,0:T(8,128)(2,1)} %param.17, f32[1024]{0:T(1024)S(1)} %slice.93, f32[4096]{0:T(1024)S(1)} %bitcast.60), kind=kLoop, calls=%fused_computation.4 | loop fusion | flops 16777216 | bytes 16797696 | tf_op jit(solution)/shard_map/convert_element_type | solution.py:287
  198.4 2.2 dynamic-slice_add_fusion
  200.7 1.5 collective-permute-start.5
  202.2 1.8 dynamic-slice_add_fusion.1
  205.9 15.2 %collective-permute-done.5 = f32[384,512]{1,0:T(8,128)S(1)} collective-permute-done((f32[384,512]{1,0:T(8,128)S(1)}, f32[384,512]{1,0:T(8,128)S(1)}, u32[]{:S(2)}, u32[]{:S(2)}) %collective-permute-start.5) | collective-permute-done | bytes 786464 | tf_op jit(solution)/shard_map/ppermute | solution.py:311
  221.1 16.5 %collective-permute-done.3 = f32[384,512]{1,0:T(8,128)S(1)} collective-permute-done((f32[384,512]{1,0:T(8,128)S(1)}, f32[384,512]{1,0:T(8,128)S(1)}, u32[]{:S(2)}, u32[]{:S(2)}) %collective-permute-start.3) | collective-permute-done | bytes 786464 | tf_op jit(solution)/shard_map/ppermute | solution.py:311
  (91 shorter events, 21.1 us)
Async XLA Ops:
  7.2 181.8 %all-reduce.3.cloned.1.call-start = ((), (), s32[]{:S(2)}) async-start(), calls=%async_computation | async-start | bytes 2621440 | tf_op jit(solution)/shard_map/psum | solution.py:264
  10.0 6.3 %copy-start = (bf16[3,128,4096]{2,1,0:T(8,128)(2,1)S(1)}, bf16[3,128,4096]{2,1,0:T(8,128)(2,1)}, u32[]{:S(2)}) copy-start(bf16[3,128,4096]{2,1,0:T(8,128)(2,1)} %param.9) | copy-start | bytes 9437188
  47.9 1.6 copy-start.3
  52.9 5.1 %copy-start.8 = (u32[32]{0:T(128)S(1)}, u32[32]{0:T(128)}, u32[]{:S(2)}) copy-start(u32[32]{0:T(128)} %constant.82) | copy-start | bytes 388
  58.0 14.1 %copy-start.5 = (f32[4096]{0:T(1024)S(1)}, f32[4096]{0:T(1024)}, u32[]{:S(2)}) copy-start(f32[4096]{0:T(1024)} %param.14) | copy-start | bytes 49156
  67.3 7.8 %copy-start.1 = (bf16[384,4,512]{2,1,0:T(4,128)(2,1)S(1)}, bf16[384,4,512]{2,1,0:T(4,128)(2,1)}, u32[]{:S(2)}) copy-start(bf16[384,4,512]{2,1,0:T(4,128)(2,1)} %get-tuple-element.25) | copy-start | bytes 4718596
  70.1 105.8 %collective-permute-start = (f32[2,384]{1,0:T(2,128)S(1)}, f32[2,384]{1,0:T(2,128)S(1)}, u32[]{:S(2)}, u32[]{:S(2)}) collective-permute-start(f32[2,384]{1,0:T(2,128)S(1)} %pad_maximum_fusion.3), channel_id=1, source_target_pairs={{0,2},{2,0},{4,6},{6,4},{8,10},{10,8},{12,14},{14,12},{1,3},{3,1},... | collective-permute-start | bytes 9224 | tf_op jit(solution)/shard_map/ppermute | solution.py:292
  176.0 2.8 %copy-start.7 = (bf16[4,512,1024]{2,1,0:T(8,128)(2,1)S(1)}, bf16[4,512,1024]{2,1,0:T(8,128)(2,1)}, u32[]{:S(2)}) copy-start(bf16[4,512,1024]{2,1,0:T(8,128)(2,1)} %get-tuple-element.15) | copy-start | bytes 12582916
  178.8 4.9 %copy-start.6 = (bf16[4,512,1024]{2,1,0:T(8,128)(2,1)S(1)}, bf16[4,512,1024]{2,1,0:T(8,128)(2,1)}, u32[]{:S(2)}) copy-start(bf16[4,512,1024]{2,1,0:T(8,128)(2,1)} %get-tuple-element.14) | copy-start | bytes 12582916
  182.2 4.9 %copy-start.4 = (f32[768,1024]{1,0:T(8,128)}, f32[768,1024]{1,0:T(8,128)S(1)}, u32[]{:S(2)}) copy-start(f32[768,1024]{1,0:T(8,128)S(1)} %fusion.21) | copy-start | bytes 9437188
  183.7 14.7 %collective-permute-start.4 = (f32[768,512]{1,0:T(8,128)}, f32[768,512]{1,0:T(8,128)}, u32[]{:S(2)}, u32[]{:S(2)}) collective-permute-start(f32[768,512]{1,0:T(8,128)} %constant_dynamic-slice_fusion), channel_id=1, source_target_pairs={{0,1},{1,0},{2,3},{3,2},{4,5},{5,4},{6,7},{7,6},{8,9},{9,8},{10,11... | collective-permute-start | bytes 4718600 | tf_op jit(solution)/shard_map/ppermute | solution.py:310
  188.4 13.8 %collective-permute-start.2 = (f32[768,512]{1,0:T(8,128)}, f32[768,512]{1,0:T(8,128)}, u32[]{:S(2)}, u32[]{:S(2)}) collective-permute-start(f32[768,512]{1,0:T(8,128)} %constant_dynamic-slice_fusion.1), channel_id=1, source_target_pairs={{0,1},{1,0},{2,3},{3,2},{4,5},{5,4},{6,7},{7,6},{8,9},{9,8},{10,11... | collective-permute-start | bytes 4718600 | tf_op jit(solution)/shard_map/ppermute | solution.py:310
  190.5 7.9 %collective-permute-start.1 = (f32[80]{0:T(128)S(1)}, f32[80]{0:T(128)S(1)}, u32[]{:S(2)}, u32[]{:S(2)}) collective-permute-start(f32[80]{0:T(128)S(1)} %multiply_reduce_fusion), channel_id=1, source_target_pairs={{0,1},{1,0},{2,3},{3,2},{4,5},{5,4},{6,7},{7,6},{8,9},{9,8},{10,11... | collective-permute-start | bytes 968 | tf_op jit(solution)/shard_map/ppermute | solution.py:318
  200.7 4.0 %copy-start.2 = (f32[80,4096]{1,0:T(8,128)S(1)}, f32[80,4096]{1,0:T(8,128)}, u32[]{:S(2)}) copy-start(f32[80,4096]{1,0:T(8,128)} %all-reduce.3.cloned.1.call-done) | copy-start | bytes 3932164
  200.7 20.4 %collective-permute-start.5 = (f32[384,512]{1,0:T(8,128)S(1)}, f32[384,512]{1,0:T(8,128)S(1)}, u32[]{:S(2)}, u32[]{:S(2)}) collective-permute-start(f32[384,512]{1,0:T(8,128)S(1)} %slice.92), channel_id=1, source_target_pairs={{0,2},{2,0},{4,6},{6,4},{8,10},{10,8},{12,14},{14,12},{1,3},{3,1},... | collective-permute-start | bytes 2359304 | tf_op jit(solution)/shard_map/ppermute | solution.py:311
  204.0 33.5 %collective-permute-start.3 = (f32[384,512]{1,0:T(8,128)S(1)}, f32[384,512]{1,0:T(8,128)S(1)}, u32[]{:S(2)}, u32[]{:S(2)}) collective-permute-start(f32[384,512]{1,0:T(8,128)S(1)} %slice.90), channel_id=1, source_target_pairs={{0,2},{2,0},{4,6},{6,4},{8,10},{10,8},{12,14},{14,12},{1,3},{3,1},... | collective-permute-start | bytes 2359304 | tf_op jit(solution)/shard_map/ppermute | solution.py:311
Sparse Core Ops, SparseCore 0:
  50.8 94.2 all-reduce.2

commit v4 on v3

--- a/solution.py
+++ b/solution.py
@@ -262,7 +262,7 @@
     picked_difference, local = direction_parts(residual, lengths, labels, earlier_means, chosen)
     local, wanted = lax.optimization_barrier((local, wanted.reshape(tokens, lines * block)))
     difference = lax.psum(local, "dp")
-    chain, crossed, neighbour_rows = chain_gather(chain_own, cross_own, wanted, lines, 4)
+    chain, crossed, neighbour_rows = chain_gather(chain_own, cross_own, wanted, lines, 8)
 
     local_square = jnp.sum(picked_difference * picked_difference)
     local_mean = local_square / half_width + 1e-06
@@ -270,24 +270,18 @@
     row_values = token_rows.astype(jnp.float32)
     matrix = out_proj[0]
     dots = jnp.sum(row_values * unit[None, :], axis=1)
-    columns = jnp.sum(matrix.astype(jnp.float32) * unit[:, None], axis=0)
-    packed = jnp.concatenate([dots, columns, local_square[None]])
+    packed = jnp.concatenate([dots, local_square[None]])
     pieces = lax.all_gather(packed, "mp")
     squares = pieces[:, -1]
     mean_dir = jnp.sum(squares) / model_width + 1e-06
     ratios = jnp.sqrt((squares / half_width + 1e-06) / mean_dir) / math.sqrt(model_width)
     sums = jnp.sum(pieces * ratios[:, None], axis=0)
     projection = sums[:tokens]
-    column_proj = sums[tokens:-1]
     refusal_dir = picked_difference * (lax.rsqrt(mean_dir) / math.sqrt(model_width))
 
     ablated = row_values - projection[:, None] * refusal_dir[None, :]
     mean_square = lax.psum(jnp.sum(ablated * ablated, axis=1), "mp") / model_width
     scale = lax.rsqrt(mean_square + 1e-05)
-    ortho_proj = (matrix.astype(jnp.float32) - refusal_dir[:, None] * column_proj[None, :]).astype(
-        jnp.bfloat16
-    )[None]
-
     stats = jnp.stack([projection, scale])
     both = jnp.concatenate([stats, lax.ppermute(stats, "dp", pair_perm(width))], axis=1)
     mine = lax.dynamic_slice_in_dim(blocked, side * block, block, 2).reshape(tokens, lines * block)
@@ -301,6 +295,14 @@
         * both[1][:, None]
         * feature_part(norm_gain).reshape(1, -1)
     ).astype(jnp.bfloat16)
+    matrix, normed = lax.optimization_barrier((matrix, normed))
+    columns = jnp.sum(matrix.astype(jnp.float32) * unit[:, None], axis=0)
+    swapped = lax.ppermute(columns, "mp", pair_perm(2))
+    column_proj = columns * ratios[core] + swapped * ratios[1 - core]
+    ortho_proj = (matrix.astype(jnp.float32) - refusal_dir[:, None] * column_proj[None, :]).astype(
+        jnp.bfloat16
+    )[None]
+
     def finish(weight):
         weight = weight.reshape(lines * block, -1)
         total = jnp.dot(normed, weight, preferred_element_type=jnp.float32)

time: 251 us -> 249 us (level)
    broadcast_in_dim x0 -> x1, other arithmetic: none -> 7.83 us  [shards(): (matrix.astype(jnp.float32) - refusal_dir[:, None] * column_proj[None, :]...]
    convert_element_type x1 -> x0, other arithmetic: 7.83 us -> none  [shards(): (matrix.astype(jnp.float32) - refusal_dir[:, None] * column_proj[None, :]...]
    reduce_sum x1, other arithmetic: 5.09 us -> 1.7 us  [shards(): columns = jnp.sum(matrix.astype(jnp.float32) * unit[:, None], axis=0)]
    unnamed x26 -> x32, local copies, waits for them, and re-layouts: 7.4 us -> 9.05 us
  transfers between devices with their start and end apart: 7 -> 8, of which waited for: 2 -> 2; matrix products, arithmetic and copies ran while one was open for 17% -> 16% of each run, Pallas kernels for 41% -> 41%
where the time goes in v4:
time: 249 us; the launch traced here: 245 us
  Pallas kernels  112 us (45%)
  other arithmetic  41.7 us (17%)
  waiting for transfers between devices  31.2 us (13%)
  local copies, waits for them, and re-layouts  25.3 us (10%)
  between operations  17.1 us (7%)
  matrix products  7.37 us (3%)
  starting transfers between devices  5.25 us (2%)
  blocking collectives  5.05 us (2%)
    pallas_call x1, Pallas kernels, chain_gather(): pl.pallas_call(functools.partial(chain_kernel, lines, parts), out_shape=(...  99.7 us
    ppermute x2, waiting for transfers between devices, finish(): result = kept[:tokens] + lax.ppermute(kept[tokens:], 'dp', pair_perm(width))  31.2 us
    pallas_call x1, Pallas kernels, gather_small(): pl.pallas_call(functools.partial(gather_kernel, peers), out_shape=jax.Sha...  11.9 us
    unnamed x32, local copies, waits for them, and re-layouts  9.05 us
    broadcast_in_dim x1, other arithmetic, shards(): (matrix.astype(jnp.float32) - refusal_dir[:, None] * column_proj[None, :]...  7.83 us
    dot_general x2, matrix products, finish(): total = jnp.dot(normed, weight, preferred_element_type=jnp.float32)  6.85 us
    another operation x1, local copies, waits for them, and re-layouts, shards(): blocked = token_rows.reshape(tokens, lines, 2 * block)  6.3 us
  transfers between devices with their start and end apart: 8, of which 2 were waited for; matrix products, arithmetic and copies ran while one was open for 16% of the time, Pallas kernels for 41%

profile of v4, /device:TPU:24, one launch (start us, length us, event | category | flops | bytes accessed | tf_op | source)
XLA Modules:
  0.0 244.6 jit_solution(2601914309867395642)
XLA Ops:
  10.1 6.3 %reshape_reshape.3 = bf16[384,4,1024]{2,1,0:T(4,128)(2,1)} reshape(bf16[3,128,4096]{2,1,0:T(8,128)(2,1)} %param.9) | data formatting | bytes 6291456 | tf_op jit(solution)/shard_map/reshape;reshape | solution.py:257
  18.0 4.7 %copy.28 = f32[1,79,2,4096]{3,1,2,0:T(8,128)} copy(f32[1,79,2,4096]{3,2,1,0:T(2,128)} %param.12) | data formatting | bytes 5177344 | tf_op args[3]
  24.7 11.9 %gather_small.1 = f32[8,72,128]{2,1,0:T(8,128)} custom-call(f32[72,128]{1,0:T(8,128)} %pad_maximum_fusion.1.mine_ref), custom_call_target="tpu_custom_call" | custom-call | tf_op jit(solution)/shard_map/gather_small/pallas_call | solution.py:87
  39.6 4.2 %fusion.7 = f32[79,4096]{1,0:T(8,128)} fusion(f32[79,2,4096]{2,0,1:T(8,128)} %bitcast.53, f32[]{:T(128)} %bitcast.6, f32[]{:T(128)} %bitcast.4), kind=kLoop, calls=%fused_computation.16 | loop fusion | flops 970752 | bytes 3883016 | tf_op jit(solution)/shard_map/sub | solution.py:44
  43.8 4.1 %constant_dynamic-slice_fusion.4 = (bf16[384,4,512]{2,1,0:T(4,128)(2,1)}, bf16[384,4,512]{2,1,0:T(4,128)(2,1)S(1)}) fusion(bf16[384,4,1024]{2,1,0:T(4,128)(2,1)} %reshape_reshape.3, s32[]{:T(128)S(6)} %select_n.85, s32[]{:T(128)S(6)} %select_n.84), kind=kLoop, calls=%fused_computation.56 | loop fusion | bytes 6291464 | tf_op jit(solution)/shard_map/dynamic_slice | solution.py:287
  47.9 1.6 copy.20
  54.9 2.4 all-reduce
  61.3 2.6 %psum.15 = f32[384]{0:T(512)S(1)} all-reduce(f32[384]{0:T(512)S(1)} %bitcast.66), channel_id=1, replica_groups=mesh['groups'=2,'dp'=8,'mp'=2] {'mp'}, use_global_device_ids=true, to_apply=%region_9.10 | all-reduce | flops 384 | bytes 3072 | tf_op jit(solution)/shard_map/psum | solution.py:283
  64.0 1.9 collective-permute-start
  65.9 3.1 %select_bitcast_fusion = (bf16[512,1024]{1,0:T(8,128)(2,1)}, bf16[512,1024]{1,0:T(8,128)(2,1)}) fusion(bf16[1,512,1024]{2,1,0:T(8,128)(2,1)} %param.16, bf16[1,512,1024]{2,1,0:T(8,128)(2,1)} %param.15, pred[]{:T(512)S(6)} %eq.34), kind=kLoop, calls=%fused_computation.20 | loop fusion | flops 1048576 | bytes 4194305 | tf_op jit(solution)/shard_map/jit(_where)/select_n | solution.py:261
  69.4 99.7 %chain_gather.1 = (bf16[4,512,1024]{2,1,0:T(8,128)(2,1)}, bf16[4,512,1024]{2,1,0:T(8,128)(2,1)}, bf16[384,2048]{1,0:T(8,128)(2,1)}) custom-call(bf16[512,1024]{1,0:T(8,128)(2,1)} %get-tuple-element.34.chain_own, bf16[512,1024]{1,0:T(8,128)(2,1)} %get-tuple-element.33.cross_own, bf16[384,2048]{1,0:T(8,128)(2,1)} %bitcast.54), custom_call_target="tpu_custom_call" | custom-call | bytes 209715200 | tf_op jit(solution)/shard_map/chain_gather/pallas_call | solution.py:227
  169.7 2.9 %multiply_convert_fusion = bf16[768,2048]{1,0:T(8,128)(2,1)S(1)} fusion(bf16[384,2048]{1,0:T(8,128)(2,1)} %get-tuple-element.14, bf16[384,2048]{1,0:T(8,128)(2,1)S(1)} %bitcast.55, f32[2048]{0:T(1024)S(1)} %bitcast.64, f32[768]{0:T(1024)S(1)} %get-tuple-element.21, f32[2048]{0:T(1024)S(1)} %bitcast.65, f32[768]{0:T(1024)S(1)} %get-tuple-element.20), kind=kLoop, calls=%fused_computation.10 | loop fusion | flops 14155776 | bytes 6313984 | tf_op jit(solution)/shard_map/convert_element_type | solution.py:297
  172.7 3.4 %fusion.22 = f32[768,1024]{1,0:T(8,128)S(1)} fusion(bf16[768,2048]{1,0:T(8,128)(2,1)S(1)} %multiply_convert_fusion, bf16[2048,1024]{1,0:T(8,128)(2,1)S(1)} %bitcast.69), kind=kOutput, calls=%fused_computation.74 | convolution fusion | flops 3221225472 | bytes 10485760 | tf_op jit(solution)/shard_map/dot_general | solution.py:308
  176.1 1.4 constant_dynamic-slice_fusion.2
  177.5 1.7 fusion
  179.7 3.4 %fusion.21 = f32[768,1024]{1,0:T(8,128)S(1)} fusion(bf16[768,2048]{1,0:T(8,128)(2,1)S(1)} %multiply_convert_fusion, bf16[2048,1024]{1,0:T(8,128)(2,1)S(1)} %bitcast.68), kind=kOutput, calls=%fused_computation.73 | convolution fusion | flops 3221225472 | bytes 10485760 | tf_op jit(solution)/shard_map/dot_general | solution.py:308
  183.2 1.6 copy-done.4
  187.4 1.5 multiply_reduce_fusion
  189.5 7.8 %fusion.2 = bf16[1,4096,1024]{2,1,0:T(8,128)(2,1)} fusion(bf16[4096,1024]{1,0:T(8,128)(2,1)} %bitcast.49, f32[1024]{0:T(1024)S(1)} %multiply_add_fusion, f32[4096]{0:T(1024)S(1)} %bitcast.63), kind=kLoop, calls=%fused_computation.4 | loop fusion | flops 16777216 | bytes 16797696 | tf_op jit(solution)/shard_map/broadcast_in_dim | solution.py:302
  197.4 1.9 dynamic-slice_add_fusion
  199.4 1.5 collective-permute-start.5
  200.9 1.8 dynamic-slice_add_fusion.1
  204.6 15.2 %collective-permute-done.5 = f32[384,512]{1,0:T(8,128)S(1)} collective-permute-done((f32[384,512]{1,0:T(8,128)S(1)}, f32[384,512]{1,0:T(8,128)S(1)}, u32[]{:S(2)}, u32[]{:S(2)}) %collective-permute-start.5) | collective-permute-done | bytes 786464 | tf_op jit(solution)/shard_map/ppermute | solution.py:313
  219.8 15.9 %collective-permute-done.3 = f32[384,512]{1,0:T(8,128)S(1)} collective-permute-done((f32[384,512]{1,0:T(8,128)S(1)}, f32[384,512]{1,0:T(8,128)S(1)}, u32[]{:S(2)}, u32[]{:S(2)}) %collective-permute-start.3) | collective-permute-done | bytes 786464 | tf_op jit(solution)/shard_map/ppermute | solution.py:313
  (101 shorter events, 24.8 us)
Async XLA Ops:
  7.2 180.3 %all-reduce.3.cloned.1.call-start = ((), (), s32[]{:S(2)}) async-start(), calls=%async_computation | async-start | bytes 2621440 | tf_op jit(solution)/shard_map/psum | solution.py:264
  10.0 6.3 %copy-start = (bf16[3,128,4096]{2,1,0:T(8,128)(2,1)S(1)}, bf16[3,128,4096]{2,1,0:T(8,128)(2,1)}, u32[]{:S(2)}) copy-start(bf16[3,128,4096]{2,1,0:T(8,128)(2,1)} %param.9) | copy-start | bytes 9437188
  47.9 1.6 copy-start.3
  49.5 3.4 %copy-start.9 = (u32[32]{0:T(128)S(1)}, u32[32]{0:T(128)}, u32[]{:S(2)}) copy-start(u32[32]{0:T(128)} %constant.86) | copy-start | bytes 388
  52.2 13.7 %copy-start.6 = (f32[4096]{0:T(1024)S(1)}, f32[4096]{0:T(1024)}, u32[]{:S(2)}) copy-start(f32[4096]{0:T(1024)} %param.14) | copy-start | bytes 49156
  61.3 7.6 %copy-start.1 = (bf16[384,4,512]{2,1,0:T(4,128)(2,1)S(1)}, bf16[384,4,512]{2,1,0:T(4,128)(2,1)}, u32[]{:S(2)}) copy-start(bf16[384,4,512]{2,1,0:T(4,128)(2,1)} %get-tuple-element.31) | copy-start | bytes 4718596
  64.0 105.7 %collective-permute-start = (f32[2,384]{1,0:T(2,128)S(1)}, f32[2,384]{1,0:T(2,128)S(1)}, u32[]{:S(2)}, u32[]{:S(2)}) collective-permute-start(f32[2,384]{1,0:T(2,128)S(1)} %pad_maximum_fusion.3), channel_id=1, source_target_pairs={{0,2},{2,0},{4,6},{6,4},{8,10},{10,8},{12,14},{14,12},{1,3},{3,1},... | collective-permute-start | bytes 9224 | tf_op jit(solution)/shard_map/ppermute | solution.py:286
  169.7 3.0 %copy-start.8 = (bf16[4,512,1024]{2,1,0:T(8,128)(2,1)S(1)}, bf16[4,512,1024]{2,1,0:T(8,128)(2,1)}, u32[]{:S(2)}) copy-start(bf16[4,512,1024]{2,1,0:T(8,128)(2,1)} %get-tuple-element.18) | copy-start | bytes 12582916
  172.6 4.8 %slice-start = ((s8[8388608]{0:T(1024)(128)(4,1)}), s8[4194304]{0:T(1024)(128)(4,1)S(1)}, s32[]{:S(2)}) async-start(s8[8388608]{0:T(1024)(128)(4,1)} %bitcast.50), calls=%async_computation.1 | async-start | bytes 8388608
  172.6 4.8 %slice-start.1 = ((s8[8388608]{0:T(1024)(128)(4,1)}), s8[4194304]{0:T(1024)(128)(4,1)S(1)}, s32[]{:S(2)}) async-start(s8[8388608]{0:T(1024)(128)(4,1)} %bitcast.50), calls=%async_computation.2 | async-start | bytes 8388608
  177.5 2.3 copy-start.7
  177.5 19.9 %collective-permute-start.4 = (f32[768,512]{1,0:T(8,128)}, f32[768,512]{1,0:T(8,128)}, u32[]{:S(2)}, u32[]{:S(2)}) collective-permute-start(f32[768,512]{1,0:T(8,128)} %constant_dynamic-slice_fusion.2), channel_id=1, source_target_pairs={{0,1},{1,0},{2,3},{3,2},{4,5},{5,4},{6,7},{7,6},{8,9},{9,8},{10,11... | collective-permute-start | bytes 4718600 | tf_op jit(solution)/shard_map/ppermute | solution.py:312
  179.2 6.9 %collective-permute-start.6 = (f32[1024]{0:T(1024)S(1)}, f32[1024]{0:T(1024)S(1)}, u32[]{:S(2)}, u32[]{:S(2)}) collective-permute-start(f32[1024]{0:T(1024)S(1)} %fusion), channel_id=1, source_target_pairs={{0,1},{1,0},{2,3},{3,2},{4,5},{5,4},{6,7},{7,6},{8,9},{9,8},{10,11... | collective-permute-start | bytes 12296 | tf_op jit(solution)/shard_map/ppermute | solution.py:300
  183.2 1.6 copy-start.4
  186.1 14.8 %collective-permute-start.2 = (f32[768,512]{1,0:T(8,128)}, f32[768,512]{1,0:T(8,128)}, u32[]{:S(2)}, u32[]{:S(2)}) collective-permute-start(f32[768,512]{1,0:T(8,128)} %constant_dynamic-slice_fusion.3), channel_id=1, source_target_pairs={{0,1},{1,0},{2,3},{3,2},{4,5},{5,4},{6,7},{7,6},{8,9},{9,8},{10,11... | collective-permute-start | bytes 4718600 | tf_op jit(solution)/shard_map/ppermute | solution.py:312
  189.0 8.4 %collective-permute-start.1 = (f32[80]{0:T(128)S(1)}, f32[80]{0:T(128)S(1)}, u32[]{:S(2)}, u32[]{:S(2)}) collective-permute-start(f32[80]{0:T(128)S(1)} %multiply_reduce_fusion), channel_id=1, source_target_pairs={{0,1},{1,0},{2,3},{3,2},{4,5},{5,4},{6,7},{7,6},{8,9},{9,8},{10,11... | collective-permute-start | bytes 968 | tf_op jit(solution)/shard_map/ppermute | solution.py:320
  197.3 3.6 %copy-start.5 = (f32[768,1024]{1,0:T(8,128)S(1)}, f32[768,1024]{1,0:T(8,128)}, u32[]{:S(2)}) copy-start(f32[768,1024]{1,0:T(8,128)} %copy-done.4) | copy-start | bytes 9437188
  199.3 4.0 %copy-start.2 = (f32[80,4096]{1,0:T(8,128)S(1)}, f32[80,4096]{1,0:T(8,128)}, u32[]{:S(2)}) copy-start(f32[80,4096]{1,0:T(8,128)} %all-reduce.3.cloned.1.call-done) | copy-start | bytes 3932164
  199.4 20.5 %collective-permute-start.5 = (f32[384,512]{1,0:T(8,128)S(1)}, f32[384,512]{1,0:T(8,128)S(1)}, u32[]{:S(2)}, u32[]{:S(2)}) collective-permute-start(f32[384,512]{1,0:T(8,128)S(1)} %slice.87), channel_id=1, source_target_pairs={{0,2},{2,0},{4,6},{6,4},{8,10},{10,8},{12,14},{14,12},{1,3},{3,1},... | collective-permute-start | bytes 2359304 | tf_op jit(solution)/shard_map/ppermute | solution.py:313
  202.7 33.0 %collective-permute-start.3 = (f32[384,512]{1,0:T(8,128)S(1)}, f32[384,512]{1,0:T(8,128)S(1)}, u32[]{:S(2)}, u32[]{:S(2)}) collective-permute-start(f32[384,512]{1,0:T(8,128)S(1)} %slice.85), channel_id=1, source_target_pairs={{0,2},{2,0},{4,6},{6,4},{8,10},{10,8},{12,14},{14,12},{1,3},{3,1},... | collective-permute-start | bytes 2359304 | tf_op jit(solution)/shard_map/ppermute | solution.py:313
Sparse Core Ops, SparseCore 0:
  50.8 95.0 all-reduce.2
